TPU v7x, 128 devices: a whole 4x4x4 slice. The times are simulated.
128 devices in a mesh: arc: 8 (over z, core), tm: 16 (over y, x).
Axes of the slice: x: 4, y: 4, z: 4, core: 2. Of those that a mesh axis runs over, the one named last changes fastest.
Arguments:
- transition: float32 [8, 6, 6, 512], P('arc', None, None, 'tm'), may hold values from -0.21 to 1.01
- forcing: bfloat16 [8, 512, 6, 9216], P('arc', 'tm'), may hold values from -0.25 to 0.25
- partials: float32 [8, 6, 512], P('arc', None, 'tm'), may hold values from -6 to 6
- observed: float32 [8, 512], P('arc', 'tm'), may hold values from -6 to 6
- counts: int32 [8, 16], P('arc', 'tm'), may hold values from 8 to 32, as said below
Outputs:
- gram: float32 [9216, 1152], P(('arc', 'tm'))
- rhs: float32 [9216], P(('arc', 'tm'))
Inputs may be any that keep to these rules, and one draw needn't show every extreme that they name: Shard (a, t) has its first counts[a, t] epochs active; in every draw some shard has all 32 active.
All inputs are finite; a program needn't handle non-finite values.
Results may differ from a plain program's by a relative error of at most 0.013.
Values may be sent and summed in bfloat16 or wider, within the bound.
No kernel may reach another device: no remote copies, remote signals or barrier semaphores. Data moves between devices by JAX's collectives and lax.ppermute only.
A program may use at most 128 MiB of HBM per device.

v0:
```python
import jax
import jax.numpy as jnp
from jax import lax
from jax.sharding import PartitionSpec as P

exact_precision = lax.Precision.HIGHEST


def prefix(shard, axis, combine, identity):
    size, here = (lax.axis_size(axis), lax.axis_index(axis))
    everything = jax.tree.map(lambda part: lax.all_gather(part, axis), shard)
    start = jax.tree.map(
        lambda part, zero: jnp.broadcast_to(jnp.asarray(zero, part.dtype), part.shape),
        shard,
        identity,
    )

    def step(k, before):
        reached = k < here
        new = combine(before, jax.tree.map(lambda part: part[k], everything))
        return jax.tree.map(lambda a, b: jnp.where(reached, a, b), new, before)

    return lax.fori_loop(0, size, step, start)


def sensitivity_rows(transition, partials):
    epochs = transition.shape[2]
    rows_total = epochs + 6
    columns = epochs + 1
    identity = jnp.eye(6, dtype=jnp.float32)
    head_rows = jnp.concatenate([partials, identity], axis=1)
    row_index = lax.broadcasted_iota(jnp.int32, (rows_total, columns), 0)
    column_index = lax.broadcasted_iota(jnp.int32, (rows_total, columns), 1) - 1
    row_limit = jnp.minimum(row_index, epochs)
    inside = column_index < row_index
    factors = jnp.where(inside, row_limit - 1 - column_index, 0)
    vectors = jnp.where(inside[None, :, :], head_rows[:, :, None], jnp.float32(0.0))
    highest = row_limit - 1
    products = transition
    stride = 1
    for bit_number in range(epochs.bit_length()):
        chosen = factors // stride % 2 == 1
        lowest = jnp.clip(highest - stride + 1, 0, epochs - 1)
        picked = jnp.take(products, lowest, axis=2)
        advanced = jnp.einsum("akl,abkl->bkl", vectors, picked, precision=exact_precision)
        vectors = jnp.where(chosen[None, :, :], advanced, vectors)
        highest = jnp.where(chosen, highest - stride, highest)
        filler = jnp.broadcast_to(identity[:, :, None], (6, 6, min(stride, epochs)))
        shifted = jnp.concatenate([products[:, :, stride:], filler], axis=2)
        products = jnp.einsum("abs,bcs->acs", shifted, products, precision=exact_precision)
        stride = stride * 2
    return vectors


def solve_small(matrix, right):
    factor = jnp.linalg.cholesky(matrix)
    halfway = lax.linalg.triangular_solve(factor, right, left_side=True, lower=True)
    return lax.linalg.triangular_solve(
        factor, halfway, left_side=True, lower=True, transpose_a=True
    )


def compose(earlier, following):
    return (
        jnp.dot(following[0], earlier[0], precision=exact_precision),
        jnp.dot(following[0], earlier[1], precision=exact_precision) + following[1],
    )


def block_product(left_rows, right_rows):
    return lax.dot_general(
        left_rows, right_rows, (((0,), (0,)), ((), ())), preferred_element_type=jnp.float32
    )


def local(transition, forcing, partials, observed, counts):
    epochs = transition.shape[3]
    coeffs = forcing.shape[3]
    vectors = sensitivity_rows(transition[0], partials[0])
    to_entry = vectors[:, :, 0]
    weights = (
        jnp.transpose(vectors[:, :, 1:], (1, 2, 0))
        .reshape(epochs + 6, epochs * 6)
        .astype(jnp.bfloat16)
    )
    local_sum = jnp.dot(
        weights, forcing[0].reshape(epochs * 6, coeffs), preferred_element_type=jnp.float32
    )
    summary_map = jnp.transpose(to_entry[:, epochs:])
    summary_forcing = local_sum[epochs:]
    identity = jnp.eye(6, dtype=jnp.float32)
    empty_forcing = jnp.zeros((6, coeffs), jnp.float32)
    entry_map, entry_forcing = prefix(
        (summary_map, summary_forcing), "tm", compose, (identity, empty_forcing)
    )
    lead_vectors = to_entry[:, :epochs]
    row_state = jnp.dot(lead_vectors.T, entry_map, precision=exact_precision)
    row_coeff = local_sum[:epochs] + jnp.dot(
        lead_vectors.T, entry_forcing, precision=exact_precision
    )
    obs_row = observed[0]
    active = lax.broadcasted_iota(jnp.int32, (epochs,), 0) < counts[0, 0]
    weighted = jnp.where(active[:, None], row_state, jnp.float32(0.0))
    information = jnp.dot(weighted.T, row_state, precision=exact_precision)
    coupling = jnp.dot(weighted.T, row_coeff, precision=exact_precision)
    coupling_obs = jnp.dot(weighted.T, obs_row, precision=exact_precision)
    information, coupling, coupling_obs = lax.psum((information, coupling, coupling_obs), "tm")
    information = information + identity
    solved = solve_small(information, coupling)
    solved_obs = solve_small(information, coupling_obs[:, None])[:, 0]
    reduced = jnp.where(
        active[:, None],
        row_coeff - jnp.dot(row_state, solved, precision=exact_precision),
        jnp.float32(0.0),
    ).astype(jnp.bfloat16)
    reduced_obs = jnp.where(
        active,
        obs_row - jnp.dot(row_state, solved_obs, precision=exact_precision),
        jnp.float32(0.0),
    ).astype(jnp.bfloat16)
    arc_count = lax.axis_size("arc")
    weighting = 1.0 / (arc_count * epochs * lax.axis_size("tm"))
    received = lax.all_to_all(reduced, "arc", split_axis=1, concat_axis=0, tiled=True)
    gram_term = block_product(received, received) * weighting
    gram_share = lax.psum_scatter(
        gram_term.astype(jnp.bfloat16), "tm", scatter_dimension=0, tiled=True
    ).astype(jnp.float32)
    rhs_term = (
        jnp.dot(reduced_obs[None, :], reduced, preferred_element_type=jnp.float32)[0] * weighting
    )
    rhs_share = lax.psum_scatter(rhs_term, ("arc", "tm"), scatter_dimension=0, tiled=True)
    return (gram_share, rhs_share)


def solution(mesh):
    return jax.shard_map(
        local,
        mesh=mesh,
        in_specs=(
            P("arc", None, None, "tm"),
            P("arc", "tm", None, None),
            P("arc", None, "tm"),
            P("arc", "tm"),
            P("arc", "tm"),
        ),
        out_specs=(P(("arc", "tm"), None), P(("arc", "tm"))),
        check_vma=False,
    )
```

profile of v0, /device:TPU:24, one launch (start us, length us, event | category | flops | bytes accessed | tf_op | source)
XLA Modules:
  0.0 435.3 jit_solution(10582203767039384938)
XLA Ops:
  10.0 5.0 %gather_fusion.5 = f32[1254,6,6]{2,1,0:T(8,128)} fusion(f32[6,6,32]{1,0,2:T(8,128)S(1)} %bitcast.215, s32[2048]{0:T(1024)S(1)} %pad_clamp_fusion), kind=kCustom, calls=%fused_computation.5.clone | custom fusion | bytes 366168 | tf_op jit(solution)/shard_map/jit(_take)/gather | solution.py:44
  15.6 5.0 %gather_fusion.4 = f32[1254,6,6]{2,1,0:T(8,128)} fusion(f32[6,6,32]{1,0,2:T(8,128)S(1)} %convolution_bitcast_fusion.5, s32[2048]{0:T(1024)S(1)} %pad_clamp_fusion.1), kind=kCustom, calls=%fused_computation.4.clone | custom fusion | bytes 366168 | tf_op jit(solution)/shard_map/jit(_take)/gather | solution.py:44
  21.3 5.0 %gather_fusion.3 = f32[1254,6,6]{1,2,0:T(8,128)} fusion(f32[6,6,32]{0,1,2:T(8,128)S(1)} %convolution_bitcast_fusion.4, s32[2048]{0:T(1024)S(1)} %pad_clamp_fusion.2), kind=kCustom, calls=%fused_computation.3.clone | custom fusion | bytes 366168 | tf_op jit(solution)/shard_map/jit(_take)/gather | solution.py:44
  27.0 5.0 %gather_fusion.2 = f32[1254,6,6]{1,2,0:T(8,128)} fusion(f32[6,6,32]{0,1,2:T(8,128)S(1)} %convolution_bitcast_fusion.3, s32[2048]{0:T(1024)S(1)} %pad_clamp_fusion.3), kind=kCustom, calls=%fused_computation.2.clone | custom fusion | bytes 366168 | tf_op jit(solution)/shard_map/jit(_take)/gather | solution.py:44
  32.5 5.0 %gather_fusion.1 = f32[1254,6,6]{1,2,0:T(8,128)} fusion(f32[6,6,32]{0,1,2:T(8,128)S(1)} %convolution_bitcast_fusion.2, s32[2048]{0:T(1024)S(1)} %pad_clamp_fusion.4), kind=kCustom, calls=%fused_computation.1.clone | custom fusion | bytes 366168 | tf_op jit(solution)/shard_map/jit(_take)/gather | solution.py:44
  38.2 11.1 %fusion.15 = f32[38,33,1,6]{3,2,1,0:T(1,128)S(1)} fusion(f32[38,33,6,6]{3,2,1,0:T(8,128)} %bitcast.220, pred[38,33]{1,0:T(8,128)(4,1)S(1)} %compare_and_fusion, f32[6,38,33,1]{0,1,2,3:T(8,128)S(1)} %select_bitcast_fusion), kind=kOutput, calls=%fused_computation.26 | convolution fusion | flops 586872 | bytes 242022 | tf_op jit(solution)/shard_map/akl,abkl->bkl/dot_general | solution.py:45
  49.7 11.5 %fusion.17 = f32[38,33,1,6]{3,2,1,0:T(1,128)S(1)} fusion(f32[38,33,6,6]{3,2,1,0:T(8,128)} %bitcast.221, pred[38,33]{1,0:T(8,128)(4,1)S(1)} %get-tuple-element.185, f32[6,38,33,1]{0,1,2,3:T(8,128)S(1)} %fusion.56), kind=kOutput, calls=%fused_computation.28 | convolution fusion | flops 586872 | bytes 242022 | tf_op jit(solution)/shard_map/akl,abkl->bkl/dot_general | solution.py:45
  61.9 11.3 %fusion.19 = f32[38,33,1,6]{3,2,1,0:T(1,128)S(1)} fusion(f32[38,33,6,6]{2,3,1,0:T(8,128)S(1)} %bitcast.224, pred[38,33]{1,0:T(8,128)(4,1)S(1)} %get-tuple-element.182, f32[6,38,33,1]{0,1,2,3:T(8,128)S(1)} %fusion.144), kind=kOutput, calls=%fused_computation.30 | convolution fusion | flops 586872 | bytes 242022 | tf_op jit(solution)/shard_map/akl,abkl->bkl/dot_general | solution.py:45
  74.1 11.3 %fusion.21 = f32[38,33,1,6]{3,2,1,0:T(1,128)S(1)} fusion(f32[38,33,6,6]{2,3,1,0:T(8,128)S(1)} %bitcast.230, pred[38,33]{1,0:T(8,128)(4,1)S(1)} %get-tuple-element.183, f32[6,38,33,1]{0,1,2,3:T(8,128)S(1)} %fusion.58), kind=kOutput, calls=%fused_computation.32 | convolution fusion | flops 586872 | bytes 242022 | tf_op jit(solution)/shard_map/akl,abkl->bkl/dot_general | solution.py:45
  86.4 11.5 %fusion.23 = f32[38,33,1,6]{3,2,1,0:T(1,128)S(1)} fusion(f32[38,33,6,6]{2,3,1,0:T(8,128)S(1)} %bitcast.227, pred[38,33]{1,0:T(8,128)(4,1)S(1)} %get-tuple-element.181, f32[6,38,33,1]{0,1,2,3:T(8,128)S(1)} %bitcast.216), kind=kOutput, calls=%fused_computation.34 | convolution fusion | flops 586872 | bytes 242022 | tf_op jit(solution)/shard_map/akl,abkl->bkl/dot_general | solution.py:45
  98.6 5.0 %gather_fusion = f32[1254,6,6]{1,2,0:T(8,128)} fusion(f32[6,6,32]{0,1,2:T(8,128)S(1)} %convolution_bitcast_fusion.1, s32[2048]{0:T(1024)S(1)} %pad_clamp_fusion.5), kind=kCustom, calls=%fused_computation.clone | custom fusion | bytes 366168 | tf_op jit(solution)/shard_map/jit(_take)/gather | solution.py:44
  103.6 11.0 %fusion.25 = f32[38,33,1,6]{3,2,1,0:T(1,128)S(1)} fusion(f32[38,33,6,6]{2,3,1,0:T(8,128)} %bitcast.231, pred[38,33]{1,0:T(8,128)(4,1)S(1)} %get-tuple-element.184, f32[6,38,33,1]{0,1,2,3:T(8,128)S(1)} %fusion.59), kind=kOutput, calls=%fused_computation.36 | convolution fusion | flops 586872 | bytes 242022 | tf_op jit(solution)/shard_map/akl,abkl->bkl/dot_general | solution.py:45
  116.9 6.1 %copy.126 = bf16[1,32,6,9216]{3,2,1,0:T(8,128)(2,1)} copy(bf16[1,32,6,9216]{3,1,2,0:T(8,128)(2,1)} %param.11) | data formatting | bytes 7077888 | tf_op args[1]
  123.0 3.7 reshape_squeeze.3
  131.7 23.4 %all-gather.2 = f32[16,6,6]{2,1,0:T(8,128)S(1)} all-gather(f32[1,6,6]{2,1,0:T(8,128)S(1)} %slice_bitcast_fusion.2), channel_id=2, replica_groups=mesh['arc'=8,'tm'=16] {'tm'}, dimensions={0}, use_global_device_ids=true | all-gather | bytes 2448 | tf_op jit(solution)/shard_map/all_gather | solution.py:11
  155.0 31.2 %all-gather.6.cloned.1.call-done = f32[16,6,9216]{2,1,0:T(8,128)} async-done(((f32[1,6,9216]{2,1,0:T(8,128)}), f32[16,6,9216]{2,1,0:T(8,128)}) %all-gather.6.cloned.1.call-update) | async-done | bytes 3538960 | tf_op jit(solution)/shard_map/all_gather | solution.py:11
  186.3 24.5 %while.16 = (s32[]{:T(128)}, f32[6,6]{1,0:T(8,128)S(1)}, f32[6,9216]{1,0:T(8,128)S(1)}, s32[]{:T(128)}, f32[16,6,6]{2,1,0:T(8,128)S(1)}, /*index=5*/f32[16,6,9216]{2,1,0:T(8,128)}, s32[]{:T(128)}, s32[]{:T(128)}) while((s32[]{:T(128)}, f32[6,6]{1,0:T(8,128)S(1)}, f32[6,9216]{1,0:T(8,128)S(1)}, s32[]{:T(128)}, ...), condition=%wide.region_1.3_spmd.clone, body=%wide.region_0.2_spmd.clone.sunk | while | flops 4205128 | bytes 1567772 | solution.py:23
  211.3 32.6 %all-reduce.2 = (f32[6,6]{0,1:T(8,128)S(1)}, f32[6]{0:T(128)S(1)}) all-reduce(f32[6,6]{0,1:T(8,128)S(1)} %fusion.106, f32[6]{0:T(128)S(1)} %convolution_bitcast_fusion.9), channel_id=1, replica_groups=mesh['arc'=8,'tm'=16] {'tm'}, use_global_device_ids=true, to_apply=%region_2.4 | all-reduce | flops 42 | bytes 336 | tf_op jit(solution)/shard_map/psum | solution.py:107
  249.1 83.7 %all-reduce.5.cloned.1.call-done = f32[6,9216]{1,0:T(8,128)} async-done(((f32[6,9216]{1,0:T(8,128)}), f32[6,9216]{1,0:T(8,128)}) %all-reduce.5.cloned.1.call-update) | async-done | bytes 221200 | tf_op jit(solution)/shard_map/psum | solution.py:107
  335.8 15.3 %all_to_all.16 = bf16[32,8,1152]{2,0,1:T(8,128)(2,1)S(1)} all-to-all(bf16[32,8,1152]{2,0,1:T(8,128)(2,1)S(1)} %bitcast.218), channel_id=1, replica_groups=mesh['arc'=8,'tm'=16] {'arc'}, dimensions={1} | all-to-all | bytes 1179648 | tf_op jit(solution)/shard_map/all_to_all | solution.py:123
  351.2 2.5 fusion.14
  354.3 63.7 %all-reduce.1 = f32[9216]{0:T(1024)S(1)} all-reduce(f32[9216]{0:T(1024)S(1)} %broadcast_multiply_fusion), channel_id=5, replica_groups=mesh['arc'=8,'tm'=16] {'arc','tm'}, use_global_device_ids=true, to_apply=%region_8.11.clone | all-reduce | flops 9216 | bytes 73728
  418.6 8.1 %reduce-scatter.4.cloned.1.call-done = bf16[72,1152]{1,0:T(8,128)(2,1)} async-done(((bf16[1152,1152]{1,0:T(8,128)(2,1)}), bf16[72,1152]{1,0:T(8,128)(2,1)}) %reduce-scatter.4.cloned.1.call-update) | async-done | bytes 165904
  426.7 1.7 convert_element_type.51
  (185 shorter events, 49.6 us)
Async XLA Ops:
  7.2 179.1 %all-gather.6.cloned.1.call-start = ((), (), s32[]{:S(2)}) async-start(), calls=%async_computation.3 | async-start | bytes 5013504 | tf_op jit(solution)/shard_map/all_gather | solution.py:11
  32.5 17.1 %copy-start = (f32[6,6,32]{0,1,2:T(8,128)}, f32[6,6,32]{0,1,2:T(8,128)S(1)}, u32[]{:S(2)}) copy-start(f32[6,6,32]{0,1,2:T(8,128)S(1)} %convolution_bitcast_fusion.2) | copy-start | bytes 13828
  49.2 12.6 %slice-start.1 = ((s8[5136384]{0:T(1024)(128)(4,1)}), s8[4194304]{0:T(1024)(128)(4,1)S(1)}, s32[]{:S(2)}) async-start(s8[5136384]{0:T(1024)(128)(4,1)} %bitcast.222), calls=%async_computation.6 | async-start | bytes 8388608
  49.7 12.2 %slice-start.2 = ((s8[5136384]{0:T(1024)(128)(4,1)}), s8[942080]{0:T(1024)(128)(4,1)S(1)}, s32[]{:S(2)}) async-start(s8[5136384]{0:T(1024)(128)(4,1)} %bitcast.222), calls=%async_computation.7 | async-start | bytes 1884160
  61.9 12.2 %slice-start.5 = ((s8[5136384]{0:T(1024)(128)(4,1)}), s8[4194304]{0:T(1024)(128)(4,1)S(1)}, s32[]{:S(2)}) async-start(s8[5136384]{0:T(1024)(128)(4,1)} %bitcast.228), calls=%async_computation.10 | async-start | bytes 8388608
  61.9 12.1 %slice-start.6 = ((s8[5136384]{0:T(1024)(128)(4,1)}), s8[942080]{0:T(1024)(128)(4,1)S(1)}, s32[]{:S(2)}) async-start(s8[5136384]{0:T(1024)(128)(4,1)} %bitcast.228), calls=%async_computation.11 | async-start | bytes 1884160
  73.2 13.1 %slice-start.3 = ((s8[5136384]{0:T(1024)(128)(4,1)}), s8[4194304]{0:T(1024)(128)(4,1)S(1)}, s32[]{:S(2)}) async-start(s8[5136384]{0:T(1024)(128)(4,1)} %bitcast.225), calls=%async_computation.8 | async-start | bytes 8388608
  74.0 12.3 %slice-start.4 = ((s8[5136384]{0:T(1024)(128)(4,1)}), s8[942080]{0:T(1024)(128)(4,1)S(1)}, s32[]{:S(2)}) async-start(s8[5136384]{0:T(1024)(128)(4,1)} %bitcast.225), calls=%async_computation.9 | async-start | bytes 1884160
  86.3 11.9 %copy-start.1 = (f32[6,6,32]{0,1,2:T(8,128)S(1)}, f32[6,6,32]{0,1,2:T(8,128)}, u32[]{:S(2)}) copy-start(f32[6,6,32]{0,1,2:T(8,128)} %copy-done) | copy-start | bytes 13828
  86.4 11.9 %slice-start = ((f32[6,6,32]{0,1,2:T(8,128)}), f32[6,6,16]{0,1,2:T(8,128)S(1)}, s32[]{:S(2)}) async-start(f32[6,6,32]{0,1,2:T(8,128)} %copy-done), calls=%async_computation.5 | async-start | bytes 131072 | tf_op jit(solution)/shard_map/slice | solution.py:49
  115.0 0.8 copy-start.4
  128.2 1.2 copy-start.2
  129.4 81.8 %copy-start.5 = (f32[1,32]{1,0:T(1,128)S(1)}, f32[1,32]{1,0:T(1,128)}, u32[]{:S(2)}) copy-start(f32[1,32]{1,0:T(1,128)} %param.13) | copy-start | bytes 388
  130.1 115.1 %copy-start.3 = (f32[38,9216]{1,0:T(8,128)S(1)}, f32[38,9216]{1,0:T(8,128)}, u32[]{:S(2)}) copy-start(f32[38,9216]{1,0:T(8,128)} %copy-done.2) | copy-start | bytes 4202500
  130.1 202.7 %all-reduce.5.cloned.1.call-start = ((), (), s32[]{:S(2)}) async-start(), calls=%async_computation.2 | async-start | bytes 589824 | tf_op jit(solution)/shard_map/psum | solution.py:107
  247.6 179.0 %reduce-scatter.4.cloned.1.call-start = ((), (), s32[]{:S(2)}) async-start(), calls=%async_computation.4 | async-start | bytes 2820096
Sparse Core Ops, SparseCore 0:
  130.2 56.0 all-gather.5
  247.8 84.9 all-reduce.4
  353.8 72.8 reduce-scatter.3
where the time goes:
time: 444 us; the launch traced here: 435 us
  blocking collectives  135 us (30%)
  waiting for transfers between devices  123 us (28%)
  matrix products  104 us (23%)
  local copies, waits for them, and re-layouts  48.7 us (11%)
  between operations  15.6 us (4%)
  other arithmetic  8.4 us (2%)
    psum x1, waiting for transfers between devices, local(): lax.psum((information, coupling, coupling_obs), 'tm')  83.7 us
    dot_general x6, matrix products, sensitivity_rows(): jnp.einsum('akl,abkl->bkl', vectors, picked, precision=exact_precision)  67.8 us
    unnamed x1, blocking collectives  63.7 us
    psum x1, blocking collectives, local(): lax.psum((information, coupling, coupling_obs), 'tm')  32.6 us
    all_gather x1, waiting for transfers between devices, prefix(): everything = jax.tree.map(lambda part: lax.all_gather(part, axis), shard)  31.2 us
    gather x6, local copies, waits for them, and re-layouts, sensitivity_rows(): picked = jnp.take(products, lowest, axis=2)  30.1 us
    all_gather x1, blocking collectives, prefix(): everything = jax.tree.map(lambda part: lax.all_gather(part, axis), shard)  23.4 us
    dot_general x16, matrix products, compose(): jnp.dot(following[0], earlier[1], precision=exact_precision) + following[1]  21.5 us
  transfers between devices with their start and end apart: 3, of which 3 were waited for; matrix products, arithmetic and copies ran while one was open for 1% of the time, Pallas kernels for 0%

commit v1 on v0

v1 whole, which is shorter than its diff:
```python
import jax
import jax.numpy as jnp
from jax import lax
from jax.experimental import pallas as pl
from jax.experimental.pallas import tpu as pltpu
from jax.sharding import PartitionSpec as P

EP = 32
BLK = 1152
HALF = 576
SLICE = 72
ROWS = 48
OUT_ROWS = 80
TS = 16
AUG = 128
WIDE = BLK + AUG
f32 = jnp.float32
bf16 = jnp.bfloat16


def rounded(x):
    return x.astype(bf16).astype(f32)


def pack_kernel(cnt_ref, tr_ref, pa_ref, ob_ref, f_hbm, out_ref, fbuf, wt_ref, w_ref, blk_ref, sm_ref, sems):
    j = pl.program_id(0)
    n_blocks = fbuf.shape[0]

    def fetch(b):
        return pltpu.make_async_copy(f_hbm.at[:, :, pl.ds(b * BLK, BLK)], fbuf.at[b], sems.at[b])

    @pl.when(j == 0)
    def _():
        for b in range(n_blocks):
            fetch(b).start()
        lane = lax.broadcasted_iota(jnp.int32, (6, 128), 1)
        sub = lax.broadcasted_iota(jnp.int32, (6, 128), 0)
        sm_ref[...] = jnp.zeros_like(sm_ref)
        sm_ref[0:6, 0:EP] = pa_ref[...]
        heads = sm_ref[0:6, :]
        rows = jnp.where(lane == sub + EP, f32(1.0), f32(0.0))
        for i in range(EP - 1, -1, -1):
            wt_ref[:, i, :] = rows
            new = None
            for c in range(6):
                term = tr_ref[c, :, i : i + 1] * rows[c : c + 1, :]
                new = term if new is None else new + term
            rows = jnp.where(lane == i, heads, new)
        sm_ref[0:6, :] = rows
        sm_ref[6:7, 0:EP] = ob_ref[...]
        lane1 = lax.broadcasted_iota(jnp.int32, (1, 128), 1)
        sm_ref[7:8, :] = jnp.where((lane1 < EP) & (lane1 < cnt_ref[0, 0]), f32(1.0), f32(0.0))
        weights = jnp.transpose(wt_ref[...].reshape(6 * EP, 128))
        w_ref[...] = weights[0:ROWS, :].astype(bf16)
        small = jnp.concatenate([sm_ref[b : b + 1, :] for b in range(8)] + [jnp.zeros((1, 128), f32)], axis=1)
        high = rounded(small)
        middle = rounded(small - high)
        blk_ref[...] = jnp.zeros_like(blk_ref)
        blk_ref[38:39, :] = high
        blk_ref[39:40, :] = middle
        blk_ref[46:47, :] = small - high - middle

    fetch(j).wait()
    local = jnp.dot(w_ref[...], fbuf[j].reshape(6 * EP, BLK), preferred_element_type=f32)
    blk_ref[0:38, :] = local[0:38, :]
    summary = local[32:38, :]
    blk_ref[40:46, :] = summary - rounded(summary)
    packed = blk_ref[...].astype(bf16)
    out_ref[0] = packed
    out_ref[1] = packed


def pack(counts, transition, partials, observed, forcing):
    n_blocks = forcing.shape[2] // BLK
    return pl.pallas_call(
        pack_kernel,
        grid=(n_blocks,),
        out_shape=jax.ShapeDtypeStruct((2 * n_blocks, ROWS, BLK), bf16),
        in_specs=[
            pl.BlockSpec(memory_space=pltpu.SMEM),
            pl.BlockSpec((6, 6, EP), lambda j: (0, 0, 0)),
            pl.BlockSpec((6, EP), lambda j: (0, 0)),
            pl.BlockSpec((1, EP), lambda j: (0, 0)),
            pl.BlockSpec(memory_space=pl.ANY),
        ],
        out_specs=pl.BlockSpec((2, ROWS, BLK), lambda j: (j, 0, 0)),
        scratch_shapes=[
            pltpu.VMEM((n_blocks, 6, EP, BLK), bf16),
            pltpu.VMEM((6, EP, 128), f32),
            pltpu.VMEM((ROWS, 6 * EP), bf16),
            pltpu.VMEM((ROWS, BLK), f32),
            pltpu.VMEM((8, 128), f32),
            pltpu.SemaphoreType.DMA((n_blocks,)),
        ],
        compiler_params=pltpu.CompilerParams(vmem_limit_bytes=32 << 20),
        name="pack_rows",
    )(counts, transition, partials, observed, forcing)


def normal_kernel(place_ref, r_ref, keep_ref, send_ref, te_ref, tt_ref, in_ref, y_ref, n_ref, x_ref, l_ref, g_ref, rr_ref):
    half = place_ref[0]
    core = place_ref[1]
    rows_of = [r_ref[t, 32:48, :].astype(f32) for t in range(TS)]
    for t in range(TS):
        both = rows_of[t][0:8, :] + rows_of[t][8:16, :]
        small = both[6:7, :] + both[7:8, :]
        for b in range(8):
            te_ref[8 * t + b : 8 * t + b + 1, :] = small[:, 128 * b : 128 * b + 128]
    turned = jnp.transpose(te_ref[...])[0:40, :]
    for t in range(TS):
        tt_ref[t] = turned if t == 0 else pltpu.roll(turned, 128 - 8 * t, 1)

    sub = lax.broadcasted_iota(jnp.int32, (8, BLK), 0)
    subw = lax.broadcasted_iota(jnp.int32, (8, WIDE), 0)
    lanew = lax.broadcasted_iota(jnp.int32, (8, WIDE), 1)
    state = jnp.where((lanew == subw + BLK) & (subw < 6), f32(1.0), f32(0.0))
    for t in range(TS):
        in_ref[t] = state
        if t == TS - 1:
            break
        both = rows_of[t][0:8, :] + rows_of[t][8:16, :]
        both = jnp.where(sub < 6, both, f32(0.0))
        new = jnp.concatenate([both, jnp.zeros((8, AUG), f32)], axis=1)
        for b in range(6):
            new = new + tt_ref[t, 32:40, b : b + 1] * state[b : b + 1, :]
        state = new

    lane_aug = lax.broadcasted_iota(jnp.int32, (EP, AUG), 1)

    def rows_step(t, carry):
        coef = tt_ref[t, 0:EP, :]
        active = coef[:, 7:8] > f32(0.5)
        base = jnp.concatenate(
            [r_ref[t, 0:EP, :].astype(f32), jnp.where(lane_aug == 6, coef[:, 6:7], f32(0.0))], axis=1
        )
        for b in range(6):
            base = base + coef[:, b : b + 1] * in_ref[t, b : b + 1, :]
        y_ref[pl.ds(pl.multiple_of(t * EP, EP), EP), :] = jnp.where(active, base, f32(0.0))
        return carry

    lax.fori_loop(0, TS, rows_step, 0)

    aug = y_ref[:, BLK:WIDE]
    lane_all = lax.broadcasted_iota(jnp.int32, aug.shape, 1)
    states = jnp.where(lane_all < 6, aug, f32(0.0))
    high = states.astype(bf16)
    low = (states - high.astype(f32)).astype(bf16)
    low_aug = (aug - rounded(aug)).astype(bf16)
    dims = (((0,), (0,)), ((), ()))
    whole = y_ref[...].astype(bf16)
    right = jnp.concatenate([whole, low_aug], axis=1)
    n_high = lax.dot_general(high, right, dims, preferred_element_type=f32)[0:8]
    n_low = lax.dot_general(low, right, dims, preferred_element_type=f32)[0:8]
    total = n_high + n_low
    augmented = total[:, BLK:WIDE] + total[:, WIDE:]
    eye = jnp.where(
        (lax.broadcasted_iota(jnp.int32, (8, AUG), 1) == lax.broadcasted_iota(jnp.int32, (8, AUG), 0)), f32(1.0), f32(0.0)
    )
    system = jnp.concatenate([total[:, 0:BLK], augmented + eye], axis=1)
    row_id = lax.broadcasted_iota(jnp.int32, (8, WIDE), 0)
    for p in range(6):
        column = system[:, BLK + p : BLK + p + 1]
        pivot = system[p : p + 1, :] / system[p : p + 1, BLK + p : BLK + p + 1]
        system = jnp.where(row_id == p, pivot, system - column * pivot)
    n_ref[...] = system

    def reduce_step(t, carry):
        at = pl.ds(pl.multiple_of(t * EP, EP), EP)
        rows = y_ref[at, :]
        coef = rows[:, BLK:WIDE]
        for b in range(6):
            rows = rows - coef[:, b : b + 1] * n_ref[b : b + 1, :]
        x_ref[at, :] = rows[:, 0:BLK].astype(bf16)
        tail = jnp.where(lane_aug == 6, rows[:, BLK:WIDE], f32(0.0))
        l_ref[at, HALF : HALF + 64] = pltpu.roll(tail, 122, 1)[:, 0:64].astype(bf16)
        return carry

    lax.fori_loop(0, TS, reduce_step, 0)

    @pl.when(half == 0)
    def _():
        l_ref[:, 0:HALF] = x_ref[:, 0:HALF]

    @pl.when(half == 1)
    def _():
        l_ref[:, 0:HALF] = x_ref[:, HALF:BLK]

    scale = f32(1.0 / 4096.0)
    g_ref[...] = lax.dot_general(l_ref[...], x_ref[...], dims, preferred_element_type=f32) * scale

    @pl.when(half == 0)
    def _():
        rr_ref[...] = g_ref[HALF : HALF + 8, 0:HALF]

    @pl.when(half == 1)
    def _():
        rr_ref[...] = g_ref[HALF : HALF + 8, HALF:BLK]

    for s in range(8):
        q, parity = s // 2, s % 2
        side = rr_ref[:, SLICE * s : SLICE * (s + 1)]
        extra = jnp.concatenate([side, jnp.zeros((8, BLK - SLICE), f32)], axis=1)
        block = jnp.concatenate([g_ref[SLICE * s : SLICE * (s + 1), :], extra], axis=0)

        @pl.when(core == parity)
        def _():
            keep_ref[q] = block

        @pl.when(core != parity)
        def _():
            send_ref[q] = block.astype(bf16)


def normals(place, received):
    return pl.pallas_call(
        normal_kernel,
        out_shape=(
            jax.ShapeDtypeStruct((4, OUT_ROWS, BLK), f32),
            jax.ShapeDtypeStruct((4, OUT_ROWS, BLK), bf16),
        ),
        in_specs=[pl.BlockSpec(memory_space=pltpu.SMEM), pl.BlockSpec(memory_space=pltpu.VMEM)],
        out_specs=(pl.BlockSpec(memory_space=pltpu.VMEM), pl.BlockSpec(memory_space=pltpu.VMEM)),
        scratch_shapes=[
            pltpu.VMEM((128, 128), f32),
            pltpu.VMEM((TS, 40, 128), f32),
            pltpu.VMEM((TS, 8, WIDE), f32),
            pltpu.VMEM((TS * EP, WIDE), f32),
            pltpu.VMEM((8, WIDE), f32),
            pltpu.VMEM((TS * EP, BLK), bf16),
            pltpu.VMEM((TS * EP, HALF + 64), bf16),
            pltpu.VMEM((HALF + 64, BLK), f32),
            pltpu.VMEM((8, HALF), f32),
        ],
        compiler_params=pltpu.CompilerParams(vmem_limit_bytes=40 << 20),
        name="normal_rows",
    )(place, received)


def local(transition, forcing, partials, observed, counts):
    packed = pack(counts, transition[0], partials[0], observed, jnp.transpose(forcing[0], (1, 0, 2)))
    received = lax.all_to_all(packed, "tm", split_axis=0, concat_axis=0, tiled=True)
    arc, tm = lax.axis_index("arc"), lax.axis_index("tm")
    place = jnp.stack([tm % 2, arc % 2]).astype(jnp.int32)
    keep, send = normals(place, received)
    arcs, shards = lax.axis_size("arc"), lax.axis_size("tm")
    other_core = [(a * shards + t, (a ^ 1) * shards + t) for a in range(arcs) for t in range(shards)]
    arrived = lax.ppermute(send, ("arc", "tm"), other_core)
    pair_sum = (keep + arrived.astype(f32)).astype(bf16)
    same_core = [[c + 2 * z for z in range(arcs // 2)] for c in range(2)]
    slices = lax.all_to_all(pair_sum, "arc", split_axis=0, concat_axis=0, tiled=True, axis_index_groups=same_core)
    mine = jnp.sum(slices.astype(f32), axis=0).astype(bf16)
    to_owner = [
        (a * shards + t, (t // 2) * shards + 8 * (t % 2) + a) for a in range(arcs) for t in range(shards)
    ]
    final = lax.ppermute(mine, ("arc", "tm"), to_owner).astype(f32)
    return final[0:SLICE, :], final[SLICE, 0:SLICE]


def solution(mesh):
    return jax.shard_map(
        local,
        mesh=mesh,
        in_specs=(
            P("arc", None, None, "tm"),
            P("arc", "tm", None, None),
            P("arc", None, "tm"),
            P("arc", "tm"),
            P("arc", "tm"),
        ),
        out_specs=(P(("arc", "tm"), None), P(("arc", "tm"))),
        check_vma=False,
    )
```

time: 444 us -> 91.8 us (0.21); the launches traced: 435 us -> 91.4 us
  blocking collectives: 135 us -> 17.2 us
  matrix products: 104 us -> 0 us
  waiting for transfers between devices: 123 us -> 39.7 us
  local copies, waits for them, and re-layouts: 48.7 us -> 5.33 us
  Pallas kernels: 0 us -> 15.7 us
  between operations: 15.6 us -> 1.32 us
  starting transfers between devices: 0.37 us -> 11.7 us
  other arithmetic: 8.4 us -> 0.4 us
    dot_general x53 -> x0, matrix products: 102 us -> none  [the longest x6 67.8 us: sensitivity_rows(): jnp.einsum('akl,abkl->bkl', vectors, picked, precision=exact_precision)]
    psum x1 -> x0, waiting for transfers between devices: 83.7 us -> none  [local(): lax.psum((information, coupling, coupling_obs), 'tm')]
    unnamed x1 -> x0, blocking collectives: 63.7 us -> none
    psum x1 -> x0, blocking collectives: 32.6 us -> none  [local(): lax.psum((information, coupling, coupling_obs), 'tm')]
    all_gather x1 -> x0, waiting for transfers between devices: 31.2 us -> none  [prefix(): everything = jax.tree.map(lambda part: lax.all_gather(part, axis), shard)]
    gather x6 -> x0, local copies, waits for them, and re-layouts: 30.1 us -> none  [sensitivity_rows(): picked = jnp.take(products, lowest, axis=2)]
    all_to_all x0 -> x1, waiting for transfers between devices: none -> 25 us  [local(): lax.all_to_all(packed, 'tm', split_axis=0, concat_axis=0, tiled=True)]
    all_gather x1 -> x0, blocking collectives: 23.4 us -> none  [prefix(): everything = jax.tree.map(lambda part: lax.all_gather(part, axis), shard)]
  transfers between devices with their start and end apart: 3 -> 3, of which waited for: 3 -> 3; matrix products, arithmetic and copies ran while one was open for 1% -> 0% of each run, Pallas kernels for 0% -> 0%
where the time goes in v1:
time: 91.8 us; the launch traced here: 91.4 us
  waiting for transfers between devices  39.7 us (43%)
  blocking collectives  17.2 us (19%)
  Pallas kernels  15.7 us (17%)
  starting transfers between devices  11.7 us (13%)
  local copies, waits for them, and re-layouts  5.33 us (6%)
  between operations  1.32 us (1%)
    all_to_all x1, waiting for transfers between devices, local(): lax.all_to_all(packed, 'tm', split_axis=0, concat_axis=0, tiled=True)  25 us
    all_to_all x1, blocking collectives, local(): lax.all_to_all(pair_sum, 'arc', split_axis=0, concat_axis=0, tiled=True,...  17.2 us
    ppermute x1, waiting for transfers between devices, local(): final = lax.ppermute(mine, ('arc', 'tm'), to_owner).astype(f32)  12.5 us
    pallas_call x1, Pallas kernels, normals(): pl.pallas_call(normal_kernel, out_shape=(jax.ShapeDtypeStruct((4, OUT_ROW...  11 us
    all_to_all x1, starting transfers between devices, local(): lax.all_to_all(packed, 'tm', split_axis=0, concat_axis=0, tiled=True)  7.18 us
    pallas_call x1, Pallas kernels, pack(): pl.pallas_call(pack_kernel, grid=(n_blocks,), out_shape=jax.ShapeDtypeStr...  4.71 us
    ppermute x1, starting transfers between devices, local(): final = lax.ppermute(mine, ('arc', 'tm'), to_owner).astype(f32)  4.46 us
    unnamed x6, local copies, waits for them, and re-layouts  4.07 us
  transfers between devices with their start and end apart: 3, of which 3 were waited for; matrix products, arithmetic and copies ran while one was open for 0% of the time, Pallas kernels for 0%

profile of v1, /device:TPU:24, one launch (start us, length us, event | category | flops | bytes accessed | tf_op | source)
XLA Modules:
  0.0 91.4 jit_solution(9377255253522294530)
XLA Ops:
  1.3 0.7 copy.12
  2.0 0.7 copy.11
  2.7 0.0 copy-start
  2.7 2.0 %copy-done = bf16[1,32,6,9216]{3,1,2,0:T(8,128)(2,1)S(1)} copy-done((bf16[1,32,6,9216]{3,1,2,0:T(8,128)(2,1)S(1)}, bf16[1,32,6,9216]{3,1,2,0:T(8,128)(2,1)}, u32[]{:S(2)}) %copy-start) | copy-done | bytes 3538968
  4.7 0.0 copy-start.1
  4.7 0.7 copy-done.1
  5.3 4.7 %pack_rows.1 = bf16[16,48,1152]{2,1,0:T(8,128)(2,1)} custom-call(s32[1,1]{1,0:T(1,128)S(6)} %copy.13.cnt_ref, f32[6,6,32]{2,1,0:T(8,128)S(1)} %bitcast.14, f32[6,32]{1,0:T(8,128)S(1)} %bitcast.15, f32[1,32]{1,0:T(1,128)S(1)} %copy-done.1, bf16[6,32,9216]{2,1,0:T(8,128)(2,1)S(1)} %bitcast.13), custom_call_target="tpu_custom_call" | custom-call | tf_op jit(solution)/shard_map/pack_rows/pallas_call | solution.py:75
  10.1 7.2 %all-to-all-start = ((bf16[16,48,1152]{2,1,0:T(8,128)(2,1)}), bf16[16,48,1152]{2,1,0:T(8,128)(2,1)S(1)}, u32[]{:S(2)}, u32[]{:S(2)}) async-start(bf16[16,48,1152]{2,1,0:T(8,128)(2,1)} %pack_rows.1), calls=%async_computation | async-start | bytes 3538944 | tf_op jit(solution)/shard_map/all_to_all | solution.py:241
  17.2 0.1 pad_add_fusion.place_ref
  17.3 25.0 %all-to-all-done.r_ref = bf16[16,48,1152]{2,1,0:T(8,128)(2,1)S(1)} async-done(((bf16[16,48,1152]{2,1,0:T(8,128)(2,1)}), bf16[16,48,1152]{2,1,0:T(8,128)(2,1)S(1)}, u32[]{:S(2)}, u32[]{:S(2)}) %all-to-all-start) | async-done | bytes 1769504 | tf_op jit(solution)/shard_map/all_to_all | solution.py:241
  42.4 11.0 %normal_rows.1 = (f32[4,80,1152]{2,1,0:T(8,128)S(1)}, bf16[4,80,1152]{2,1,0:T(8,128)(2,1)S(1)}) custom-call(s32[2]{0:T(128)S(1)} %pad_add_fusion.place_ref, bf16[16,48,1152]{2,1,0:T(8,128)(2,1)S(1)} %all-to-all-done.r_ref), custom_call_target="tpu_custom_call" | custom-call | tf_op jit(solution)/shard_map/normal_rows/pallas_call | solution.py:215
  53.4 0.1 collective-permute-start
  53.5 2.2 %collective-permute-done = bf16[4,80,1152]{2,1,0:T(8,128)(2,1)S(1)} collective-permute-done((bf16[4,80,1152]{2,1,0:T(8,128)(2,1)S(1)}, bf16[4,80,1152]{2,1,0:T(8,128)(2,1)S(1)}, u32[]{:S(2)}, u32[]{:S(2)}) %collective-permute-start) | collective-permute-done | bytes 737312 | tf_op jit(solution)/shard_map/ppermute | solution.py:247
  55.7 0.2 add_convert_fusion
  55.9 17.2 %all_to_all.10 = bf16[4,80,1152]{2,1,0:T(8,128)(2,1)S(1)} all-to-all(bf16[4,80,1152]{2,1,0:T(8,128)(2,1)S(1)} %add_convert_fusion), channel_id=1, replica_groups={{0,32,64,96},{16,48,80,112},{1,33,65,97},{17,49,81,113},{2,34,66,98},{1..., dimensions={0} | all-to-all | bytes 1474560 | tf_op jit(solution)/shard_map/all_to_all | solution.py:250
  73.1 0.1 reduce_sum.12
  73.2 4.5 %collective-permute-start.1 = (bf16[80,1152]{1,0:T(8,128)(2,1)S(1)}, bf16[80,1152]{1,0:T(8,128)(2,1)S(1)}, u32[]{:S(2)}, u32[]{:S(2)}) collective-permute-start(bf16[80,1152]{1,0:T(8,128)(2,1)S(1)} %reduce_sum.12), channel_id=1, source_target_pairs={{0,0},{1,8},{2,16},{3,24},{4,32},{5,40},{6,48},{7,56},{8,64},{9,72... | collective-permute-start | bytes 552968 | tf_op jit(solution)/shard_map/ppermute | solution.py:255
  77.6 12.5 %collective-permute-done.1 = bf16[80,1152]{1,0:T(8,128)(2,1)S(1)} collective-permute-done((bf16[80,1152]{1,0:T(8,128)(2,1)S(1)}, bf16[80,1152]{1,0:T(8,128)(2,1)S(1)}, u32[]{:S(2)}, u32[]{:S(2)}) %collective-permute-start.1) | collective-permute-done | bytes 184352 | tf_op jit(solution)/shard_map/ppermute | solution.py:255
  90.1 0.5 slice_bitcast_fusion
  90.7 0.7 slice.8
  (1 shorter events, 0.0 us)
Async XLA Ops:
  2.7 2.0 %copy-start = (bf16[1,32,6,9216]{3,1,2,0:T(8,128)(2,1)S(1)}, bf16[1,32,6,9216]{3,1,2,0:T(8,128)(2,1)}, u32[]{:S(2)}) copy-start(bf16[1,32,6,9216]{3,1,2,0:T(8,128)(2,1)} %param.6) | copy-start | bytes 10616836
  4.7 0.7 copy-start.1
  10.1 32.3 %all-to-all-start = ((bf16[16,48,1152]{2,1,0:T(8,128)(2,1)}), bf16[16,48,1152]{2,1,0:T(8,128)(2,1)S(1)}, u32[]{:S(2)}, u32[]{:S(2)}) async-start(bf16[16,48,1152]{2,1,0:T(8,128)(2,1)} %pack_rows.1), calls=%async_computation | async-start | bytes 3538944 | tf_op jit(solution)/shard_map/all_to_all | solution.py:241
  53.4 2.3 %collective-permute-start = (bf16[4,80,1152]{2,1,0:T(8,128)(2,1)S(1)}, bf16[4,80,1152]{2,1,0:T(8,128)(2,1)S(1)}, u32[]{:S(2)}, u32[]{:S(2)}) collective-permute-start(bf16[4,80,1152]{2,1,0:T(8,128)(2,1)S(1)} %get-tuple-element.5), channel_id=1, source_target_pairs={{0,16},{1,17},{2,18},{3,19},{4,20},{5,21},{6,22},{7,23},{8,24},{9,... | collective-permute-start | bytes 2211848 | tf_op jit(solution)/shard_map/ppermute | solution.py:247
  73.2 16.9 %collective-permute-start.1 = (bf16[80,1152]{1,0:T(8,128)(2,1)S(1)}, bf16[80,1152]{1,0:T(8,128)(2,1)S(1)}, u32[]{:S(2)}, u32[]{:S(2)}) collective-permute-start(bf16[80,1152]{1,0:T(8,128)(2,1)S(1)} %reduce_sum.12), channel_id=1, source_target_pairs={{0,0},{1,8},{2,16},{3,24},{4,32},{5,40},{6,48},{7,56},{8,64},{9,72... | collective-permute-start | bytes 552968 | tf_op jit(solution)/shard_map/ppermute | solution.py:255

commit v2 on v1

--- a/solution.py
+++ b/solution.py
@@ -9,7 +9,7 @@
 BLK = 1152
 HALF = 576
 SLICE = 72
-ROWS = 48
+ROWS = 40
 OUT_ROWS = 80
 TS = 16
 AUG = 128
@@ -22,7 +22,10 @@
     return x.astype(bf16).astype(f32)
 
 
-def pack_kernel(cnt_ref, tr_ref, pa_ref, ob_ref, f_hbm, out_ref, fbuf, wt_ref, w_ref, blk_ref, sm_ref, sems):
+def pack_kernel(
+    cnt_ref, tr_hbm, pa_hbm, ob_hbm, f_hbm, out_ref,
+    tr_ref, pa_ref, ob_ref, fbuf, wt_ref, w_ref, blk_ref, sm_ref, sems, small_sems,
+):
     j = pl.program_id(0)
     n_blocks = fbuf.shape[0]
 
@@ -31,20 +34,29 @@
 
     @pl.when(j == 0)
     def _():
+        smalls = [
+            pltpu.make_async_copy(src, dst, small_sems.at[n])
+            for n, (src, dst) in enumerate(((tr_hbm, tr_ref), (pa_hbm, pa_ref), (ob_hbm, ob_ref)))
+        ]
+        for copy in smalls:
+            copy.start()
         for b in range(n_blocks):
             fetch(b).start()
         lane = lax.broadcasted_iota(jnp.int32, (6, 128), 1)
         sub = lax.broadcasted_iota(jnp.int32, (6, 128), 0)
         sm_ref[...] = jnp.zeros_like(sm_ref)
-        sm_ref[0:6, 0:EP] = pa_ref[...]
+        blk_ref[...] = jnp.zeros_like(blk_ref)
+        for copy in smalls:
+            copy.wait()
+        for b in range(6):
+            sm_ref[b : b + 1, 0:EP] = pa_ref[b]
         heads = sm_ref[0:6, :]
         rows = jnp.where(lane == sub + EP, f32(1.0), f32(0.0))
+        steps = [tr_ref[c, :, 0, :] for c in range(6)]
         for i in range(EP - 1, -1, -1):
             wt_ref[:, i, :] = rows
-            new = None
-            for c in range(6):
-                term = tr_ref[c, :, i : i + 1] * rows[c : c + 1, :]
-                new = term if new is None else new + term
+            terms = [steps[c][:, i : i + 1] * rows[c : c + 1, :] for c in range(6)]
+            new = ((terms[0] + terms[1]) + (terms[2] + terms[3])) + (terms[4] + terms[5])
             rows = jnp.where(lane == i, heads, new)
         sm_ref[0:6, :] = rows
         sm_ref[6:7, 0:EP] = ob_ref[...]
@@ -54,56 +66,50 @@
         w_ref[...] = weights[0:ROWS, :].astype(bf16)
         small = jnp.concatenate([sm_ref[b : b + 1, :] for b in range(8)] + [jnp.zeros((1, 128), f32)], axis=1)
         high = rounded(small)
-        middle = rounded(small - high)
-        blk_ref[...] = jnp.zeros_like(blk_ref)
         blk_ref[38:39, :] = high
-        blk_ref[39:40, :] = middle
-        blk_ref[46:47, :] = small - high - middle
+        blk_ref[39:40, :] = small - high
 
     fetch(j).wait()
     local = jnp.dot(w_ref[...], fbuf[j].reshape(6 * EP, BLK), preferred_element_type=f32)
     blk_ref[0:38, :] = local[0:38, :]
-    summary = local[32:38, :]
-    blk_ref[40:46, :] = summary - rounded(summary)
     packed = blk_ref[...].astype(bf16)
-    out_ref[0] = packed
-    out_ref[1] = packed
+    out_ref[0, 0, 0] = packed
+    out_ref[0, 1, 0] = packed
 
 
 def pack(counts, transition, partials, observed, forcing):
     n_blocks = forcing.shape[2] // BLK
+    hbm = pl.BlockSpec(memory_space=pl.ANY)
     return pl.pallas_call(
         pack_kernel,
         grid=(n_blocks,),
-        out_shape=jax.ShapeDtypeStruct((2 * n_blocks, ROWS, BLK), bf16),
-        in_specs=[
-            pl.BlockSpec(memory_space=pltpu.SMEM),
-            pl.BlockSpec((6, 6, EP), lambda j: (0, 0, 0)),
-            pl.BlockSpec((6, EP), lambda j: (0, 0)),
-            pl.BlockSpec((1, EP), lambda j: (0, 0)),
-            pl.BlockSpec(memory_space=pl.ANY),
-        ],
-        out_specs=pl.BlockSpec((2, ROWS, BLK), lambda j: (j, 0, 0)),
+        out_shape=jax.ShapeDtypeStruct((n_blocks // 2, 2, 2, ROWS, BLK), bf16),
+        in_specs=[pl.BlockSpec(memory_space=pltpu.SMEM), hbm, hbm, hbm, hbm],
+        out_specs=pl.BlockSpec((1, 2, 1, ROWS, BLK), lambda j: (j // 2, 0, j % 2, 0, 0)),
         scratch_shapes=[
+            pltpu.VMEM((6, 6, 1, EP), f32),
+            pltpu.VMEM((6, 1, EP), f32),
+            pltpu.VMEM((1, EP), f32),
             pltpu.VMEM((n_blocks, 6, EP, BLK), bf16),
             pltpu.VMEM((6, EP, 128), f32),
             pltpu.VMEM((ROWS, 6 * EP), bf16),
             pltpu.VMEM((ROWS, BLK), f32),
             pltpu.VMEM((8, 128), f32),
             pltpu.SemaphoreType.DMA((n_blocks,)),
+            pltpu.SemaphoreType.DMA((3,)),
         ],
-        compiler_params=pltpu.CompilerParams(vmem_limit_bytes=32 << 20),
+        compiler_params=pltpu.CompilerParams(vmem_limit_bytes=58 << 20),
         name="pack_rows",
-    )(counts, transition, partials, observed, forcing)
+    )(counts, transition, partials, observed, forcing).reshape(2 * n_blocks, ROWS, BLK)
 
 
 def normal_kernel(place_ref, r_ref, keep_ref, send_ref, te_ref, tt_ref, in_ref, y_ref, n_ref, x_ref, l_ref, g_ref, rr_ref):
     half = place_ref[0]
     core = place_ref[1]
-    rows_of = [r_ref[t, 32:48, :].astype(f32) for t in range(TS)]
+    turn = place_ref[2]
+    rows_of = [r_ref[t, 32:40, :].astype(f32) for t in range(TS)]
     for t in range(TS):
-        both = rows_of[t][0:8, :] + rows_of[t][8:16, :]
-        small = both[6:7, :] + both[7:8, :]
+        small = rows_of[t][6:7, :] + rows_of[t][7:8, :]
         for b in range(8):
             te_ref[8 * t + b : 8 * t + b + 1, :] = small[:, 128 * b : 128 * b + 128]
     turned = jnp.transpose(te_ref[...])[0:40, :]
@@ -118,8 +124,7 @@
         in_ref[t] = state
         if t == TS - 1:
             break
-        both = rows_of[t][0:8, :] + rows_of[t][8:16, :]
-        both = jnp.where(sub < 6, both, f32(0.0))
+        both = jnp.where(sub < 6, rows_of[t], f32(0.0))
         new = jnp.concatenate([both, jnp.zeros((8, AUG), f32)], axis=1)
         for b in range(6):
             new = new + tt_ref[t, 32:40, b : b + 1] * state[b : b + 1, :]
@@ -177,38 +182,39 @@
 
     lax.fori_loop(0, TS, reduce_step, 0)
 
-    @pl.when(half == 0)
-    def _():
-        l_ref[:, 0:HALF] = x_ref[:, 0:HALF]
-
-    @pl.when(half == 1)
-    def _():
-        l_ref[:, 0:HALF] = x_ref[:, HALF:BLK]
+    for side in range(2):
+
+        @pl.when(half == side)
+        def _():
+            for q in range(4):
+                l_ref[:, 2 * SLICE * q : 2 * SLICE * (q + 1)] = x_ref[
+                    :, 4 * SLICE * q + 2 * SLICE * side : 4 * SLICE * q + 2 * SLICE * (side + 1)
+                ]
 
     scale = f32(1.0 / 4096.0)
     g_ref[...] = lax.dot_general(l_ref[...], x_ref[...], dims, preferred_element_type=f32) * scale
 
-    @pl.when(half == 0)
-    def _():
-        rr_ref[...] = g_ref[HALF : HALF + 8, 0:HALF]
-
-    @pl.when(half == 1)
-    def _():
-        rr_ref[...] = g_ref[HALF : HALF + 8, HALF:BLK]
+    for side in range(2):
+
+        @pl.when(half == side)
+        def _():
+            for q in range(4):
+                first = 4 * SLICE * q + 2 * SLICE * side
+                rr_ref[:, 2 * SLICE * q : 2 * SLICE * (q + 1)] = g_ref[HALF : HALF + 8, first : first + 2 * SLICE]
 
     for s in range(8):
-        q, parity = s // 2, s % 2
-        side = rr_ref[:, SLICE * s : SLICE * (s + 1)]
-        extra = jnp.concatenate([side, jnp.zeros((8, BLK - SLICE), f32)], axis=1)
+        slot, parity = lax.rem(s // 2 + 4 - turn, 4), s % 2
+        beside = rr_ref[:, SLICE * s : SLICE * (s + 1)]
+        extra = jnp.concatenate([beside, jnp.zeros((8, BLK - SLICE), f32)], axis=1)
         block = jnp.concatenate([g_ref[SLICE * s : SLICE * (s + 1), :], extra], axis=0)
 
         @pl.when(core == parity)
         def _():
-            keep_ref[q] = block
+            keep_ref[slot] = block
 
         @pl.when(core != parity)
         def _():
-            send_ref[q] = block.astype(bf16)
+            send_ref[slot] = block.astype(bf16)
 
 
 def normals(place, received):
@@ -237,10 +243,16 @@
 
 
 def local(transition, forcing, partials, observed, counts):
-    packed = pack(counts, transition[0], partials[0], observed, jnp.transpose(forcing[0], (1, 0, 2)))
+    packed = pack(
+        counts,
+        jnp.transpose(transition, (1, 2, 0, 3)),
+        jnp.transpose(partials, (1, 0, 2)),
+        observed,
+        jnp.transpose(forcing[0], (1, 0, 2)),
+    )
     received = lax.all_to_all(packed, "tm", split_axis=0, concat_axis=0, tiled=True)
     arc, tm = lax.axis_index("arc"), lax.axis_index("tm")
-    place = jnp.stack([tm % 2, arc % 2]).astype(jnp.int32)
+    place = jnp.stack([tm % 4 // 2, arc % 2, tm // 4]).astype(jnp.int32)
     keep, send = normals(place, received)
     arcs, shards = lax.axis_size("arc"), lax.axis_size("tm")
     other_core = [(a * shards + t, (a ^ 1) * shards + t) for a in range(arcs) for t in range(shards)]
@@ -249,9 +261,11 @@
     same_core = [[c + 2 * z for z in range(arcs // 2)] for c in range(2)]
     slices = lax.all_to_all(pair_sum, "arc", split_axis=0, concat_axis=0, tiled=True, axis_index_groups=same_core)
     mine = jnp.sum(slices.astype(f32), axis=0).astype(bf16)
-    to_owner = [
-        (a * shards + t, (t // 2) * shards + 8 * (t % 2) + a) for a in range(arcs) for t in range(shards)
-    ]
+    to_owner = []
+    for a in range(arcs):
+        for t in range(shards):
+            z, c, y, h, odd = a // 2, a % 2, t // 4, t % 4 // 2, t % 2
+            to_owner.append((a * shards + t, (2 * y + odd) * shards + (y + z) % 4 * 4 + 2 * h + c))
     final = lax.ppermute(mine, ("arc", "tm"), to_owner).astype(f32)
     return final[0:SLICE, :], final[SLICE, 0:SLICE]
 

time: 91.8 us -> 81.7 us (0.89)
  waiting for transfers between devices: 39.7 us -> 32.3 us
  local copies, waits for them, and re-layouts: 5.33 us -> 1.26 us
  Pallas kernels: 15.7 us -> 18.3 us
  starting transfers between devices: 11.7 us -> 10.3 us
    unnamed x6 -> x0, local copies, waits for them, and re-layouts: 4.07 us -> none
    all_to_all x1, waiting for transfers between devices: 25 us -> 21 us  [local(): lax.all_to_all(packed, 'tm', split_axis=0, concat_axis=0, tiled=True)]
    ppermute x1, waiting for transfers between devices: 12.5 us -> 9.1 us  [local(): final = lax.ppermute(mine, ('arc', 'tm'), to_owner).astype(f32)]
    pallas_call x1, Pallas kernels: 4.71 us -> 7.02 us  [pack(): pl.pallas_call(pack_kernel, grid=(n_blocks,), out_shape=jax.ShapeDtypeStr...]
    ppermute x1, starting transfers between devices: 4.46 us -> 3.08 us  [local(): final = lax.ppermute(mine, ('arc', 'tm'), to_owner).astype(f32)]
where the time goes in v2:
time: 81.7 us; the launch traced here: 81 us
  waiting for transfers between devices  32.3 us (40%)
  Pallas kernels  18.3 us (22%)
  blocking collectives  17.2 us (21%)
  starting transfers between devices  10.3 us (13%)
  between operations  1.32 us (2%)
  local copies, waits for them, and re-layouts  1.26 us (2%)
    all_to_all x1, waiting for transfers between devices, local(): lax.all_to_all(packed, 'tm', split_axis=0, concat_axis=0, tiled=True)  21 us
    all_to_all x1, blocking collectives, local(): lax.all_to_all(pair_sum, 'arc', split_axis=0, concat_axis=0, tiled=True,...  17.2 us
    pallas_call x1, Pallas kernels, normals(): pl.pallas_call(normal_kernel, out_shape=(jax.ShapeDtypeStruct((4, OUT_ROW...  11.3 us
    ppermute x1, waiting for transfers between devices, local(): final = lax.ppermute(mine, ('arc', 'tm'), to_owner).astype(f32)  9.1 us
    all_to_all x1, starting transfers between devices, local(): lax.all_to_all(packed, 'tm', split_axis=0, concat_axis=0, tiled=True)  7.18 us
    pallas_call x1, Pallas kernels, pack(): pl.pallas_call(pack_kernel, grid=(n_blocks,), out_shape=jax.ShapeDtypeStr...  7.02 us
    ppermute x1, starting transfers between devices, local(): final = lax.ppermute(mine, ('arc', 'tm'), to_owner).astype(f32)  3.08 us
    ppermute x1, waiting for transfers between devices, local(): arrived = lax.ppermute(send, ('arc', 'tm'), other_core)  2.2 us
  transfers between devices with their start and end apart: 3, of which 3 were waited for; matrix products, arithmetic and copies ran while one was open for 0% of the time, Pallas kernels for 0%

profile of v2, /device:TPU:24, one launch (start us, length us, event | category | flops | bytes accessed | tf_op | source)
XLA Modules:
  0.0 81.0 jit_solution(9229558784393830281)
XLA Ops:
  1.3 7.0 %pack_rows.1 = bf16[4,2,2,40,1152]{4,3,2,1,0:T(8,128)(2,1)} custom-call(s32[1,1]{1,0:T(1,128)S(6)} %copy.7.cnt_ref, f32[6,6,1,32]{3,2,1,0:T(1,128)} %bitcast.13, f32[6,1,32]{2,1,0:T(1,128)} %bitcast.14, f32[1,32]{1,0:T(1,128)} %ob_hbm.1, bf16[6,32,9216]{2,1,0:T(8,128)(2,1)} %bitcast.12), custom_call_target="tpu_custom_call" | custom-call | tf_op jit(solution)/shard_map/pack_rows/pallas_call | solution.py:83
  8.3 7.2 %all-to-all-start = ((bf16[16,40,1152]{2,1,0:T(8,128)(2,1)}), bf16[16,40,1152]{2,1,0:T(8,128)(2,1)S(1)}, u32[]{:S(2)}, u32[]{:S(2)}) async-start(bf16[16,40,1152]{2,1,0:T(8,128)(2,1)} %bitcast.11), calls=%async_computation | async-start | bytes 2949120 | tf_op jit(solution)/shard_map/all_to_all | solution.py:253
  15.5 0.1 pad_add_fusion.place_ref
  15.6 21.0 %all-to-all-done.r_ref = bf16[16,40,1152]{2,1,0:T(8,128)(2,1)S(1)} async-done(((bf16[16,40,1152]{2,1,0:T(8,128)(2,1)}), bf16[16,40,1152]{2,1,0:T(8,128)(2,1)S(1)}, u32[]{:S(2)}, u32[]{:S(2)}) %all-to-all-start) | async-done | bytes 1474592 | tf_op jit(solution)/shard_map/all_to_all | solution.py:253
  36.5 11.3 %normal_rows.1 = (f32[4,80,1152]{2,1,0:T(8,128)S(1)}, bf16[4,80,1152]{2,1,0:T(8,128)(2,1)S(1)}) custom-call(s32[3]{0:T(128)S(1)} %pad_add_fusion.place_ref, bf16[16,40,1152]{2,1,0:T(8,128)(2,1)S(1)} %all-to-all-done.r_ref), custom_call_target="tpu_custom_call" | custom-call | tf_op jit(solution)/shard_map/normal_rows/pallas_call | solution.py:221
  47.8 0.1 collective-permute-start
  47.9 2.2 %collective-permute-done = bf16[4,80,1152]{2,1,0:T(8,128)(2,1)S(1)} collective-permute-done((bf16[4,80,1152]{2,1,0:T(8,128)(2,1)S(1)}, bf16[4,80,1152]{2,1,0:T(8,128)(2,1)S(1)}, u32[]{:S(2)}, u32[]{:S(2)}) %collective-permute-start) | collective-permute-done | bytes 737312 | tf_op jit(solution)/shard_map/ppermute | solution.py:259
  50.1 0.1 add_convert_fusion
  50.3 17.2 %all_to_all.10 = bf16[4,80,1152]{2,1,0:T(8,128)(2,1)S(1)} all-to-all(bf16[4,80,1152]{2,1,0:T(8,128)(2,1)S(1)} %add_convert_fusion), channel_id=1, replica_groups={{0,32,64,96},{16,48,80,112},{1,33,65,97},{17,49,81,113},{2,34,66,98},{1..., dimensions={0} | all-to-all | bytes 1474560 | tf_op jit(solution)/shard_map/all_to_all | solution.py:262
  67.4 0.1 reduce_sum.12
  67.6 3.1 %collective-permute-start.1 = (bf16[80,1152]{1,0:T(8,128)(2,1)S(1)}, bf16[80,1152]{1,0:T(8,128)(2,1)S(1)}, u32[]{:S(2)}, u32[]{:S(2)}) collective-permute-start(bf16[80,1152]{1,0:T(8,128)(2,1)S(1)} %reduce_sum.12), channel_id=1, source_target_pairs={{0,0},{1,16},{2,2},{3,18},{4,36},{5,52},{6,38},{7,54},{8,72},{9,88... | collective-permute-start | bytes 552968 | tf_op jit(solution)/shard_map/ppermute | solution.py:269
  70.6 9.1 %collective-permute-done.1 = bf16[80,1152]{1,0:T(8,128)(2,1)S(1)} collective-permute-done((bf16[80,1152]{1,0:T(8,128)(2,1)S(1)}, bf16[80,1152]{1,0:T(8,128)(2,1)S(1)}, u32[]{:S(2)}, u32[]{:S(2)}) %collective-permute-start.1) | collective-permute-done | bytes 184352 | tf_op jit(solution)/shard_map/ppermute | solution.py:269
  79.8 0.5 slice_bitcast_fusion
  80.3 0.7 slice.8
  (1 shorter events, 0.0 us)
Async XLA Ops:
  8.3 28.2 %all-to-all-start = ((bf16[16,40,1152]{2,1,0:T(8,128)(2,1)}), bf16[16,40,1152]{2,1,0:T(8,128)(2,1)S(1)}, u32[]{:S(2)}, u32[]{:S(2)}) async-start(bf16[16,40,1152]{2,1,0:T(8,128)(2,1)} %bitcast.11), calls=%async_computation | async-start | bytes 2949120 | tf_op jit(solution)/shard_map/all_to_all | solution.py:253
  47.8 2.3 %collective-permute-start = (bf16[4,80,1152]{2,1,0:T(8,128)(2,1)S(1)}, bf16[4,80,1152]{2,1,0:T(8,128)(2,1)S(1)}, u32[]{:S(2)}, u32[]{:S(2)}) collective-permute-start(bf16[4,80,1152]{2,1,0:T(8,128)(2,1)S(1)} %get-tuple-element.5), channel_id=1, source_target_pairs={{0,16},{1,17},{2,18},{3,19},{4,20},{5,21},{6,22},{7,23},{8,24},{9,... | collective-permute-start | bytes 2211848 | tf_op jit(solution)/shard_map/ppermute | solution.py:259
  67.6 12.2 %collective-permute-start.1 = (bf16[80,1152]{1,0:T(8,128)(2,1)S(1)}, bf16[80,1152]{1,0:T(8,128)(2,1)S(1)}, u32[]{:S(2)}, u32[]{:S(2)}) collective-permute-start(bf16[80,1152]{1,0:T(8,128)(2,1)S(1)} %reduce_sum.12), channel_id=1, source_target_pairs={{0,0},{1,16},{2,2},{3,18},{4,36},{5,52},{6,38},{7,54},{8,72},{9,88... | collective-permute-start | bytes 552968 | tf_op jit(solution)/shard_map/ppermute | solution.py:269

commit v3 on v2

--- a/solution.py
+++ b/solution.py
@@ -23,90 +23,80 @@
 
 
 def pack_kernel(
-    cnt_ref, tr_hbm, pa_hbm, ob_hbm, f_hbm, out_ref,
-    tr_ref, pa_ref, ob_ref, fbuf, wt_ref, w_ref, blk_ref, sm_ref, sems, small_sems,
+    cnt_ref, tr_hbm, pa_hbm, ob_hbm, f_hbm, out_ref, tr_ref, pa_ref, ob_ref, fbuf, wt_ref, sm_ref, sems, small_sems
 ):
-    j = pl.program_id(0)
     n_blocks = fbuf.shape[0]
-
-    def fetch(b):
-        return pltpu.make_async_copy(f_hbm.at[:, :, pl.ds(b * BLK, BLK)], fbuf.at[b], sems.at[b])
-
-    @pl.when(j == 0)
-    def _():
-        smalls = [
-            pltpu.make_async_copy(src, dst, small_sems.at[n])
-            for n, (src, dst) in enumerate(((tr_hbm, tr_ref), (pa_hbm, pa_ref), (ob_hbm, ob_ref)))
-        ]
-        for copy in smalls:
-            copy.start()
-        for b in range(n_blocks):
-            fetch(b).start()
-        lane = lax.broadcasted_iota(jnp.int32, (6, 128), 1)
-        sub = lax.broadcasted_iota(jnp.int32, (6, 128), 0)
-        sm_ref[...] = jnp.zeros_like(sm_ref)
-        blk_ref[...] = jnp.zeros_like(blk_ref)
-        for copy in smalls:
-            copy.wait()
-        for b in range(6):
-            sm_ref[b : b + 1, 0:EP] = pa_ref[b]
-        heads = sm_ref[0:6, :]
-        rows = jnp.where(lane == sub + EP, f32(1.0), f32(0.0))
-        steps = [tr_ref[c, :, 0, :] for c in range(6)]
-        for i in range(EP - 1, -1, -1):
-            wt_ref[:, i, :] = rows
-            terms = [steps[c][:, i : i + 1] * rows[c : c + 1, :] for c in range(6)]
-            new = ((terms[0] + terms[1]) + (terms[2] + terms[3])) + (terms[4] + terms[5])
-            rows = jnp.where(lane == i, heads, new)
-        sm_ref[0:6, :] = rows
-        sm_ref[6:7, 0:EP] = ob_ref[...]
-        lane1 = lax.broadcasted_iota(jnp.int32, (1, 128), 1)
-        sm_ref[7:8, :] = jnp.where((lane1 < EP) & (lane1 < cnt_ref[0, 0]), f32(1.0), f32(0.0))
-        weights = jnp.transpose(wt_ref[...].reshape(6 * EP, 128))
-        w_ref[...] = weights[0:ROWS, :].astype(bf16)
-        small = jnp.concatenate([sm_ref[b : b + 1, :] for b in range(8)] + [jnp.zeros((1, 128), f32)], axis=1)
-        high = rounded(small)
-        blk_ref[38:39, :] = high
-        blk_ref[39:40, :] = small - high
-
-    fetch(j).wait()
-    local = jnp.dot(w_ref[...], fbuf[j].reshape(6 * EP, BLK), preferred_element_type=f32)
-    blk_ref[0:38, :] = local[0:38, :]
-    packed = blk_ref[...].astype(bf16)
-    out_ref[0, 0, 0] = packed
-    out_ref[0, 1, 0] = packed
+    smalls = [
+        pltpu.make_async_copy(src, dst, small_sems.at[n])
+        for n, (src, dst) in enumerate(((tr_hbm, tr_ref), (pa_hbm, pa_ref), (ob_hbm, ob_ref)))
+    ]
+    for copy in smalls:
+        copy.start()
+    fetches = [
+        pltpu.make_async_copy(f_hbm.at[:, :, pl.ds(b * BLK, BLK)], fbuf.at[b], sems.at[b]) for b in range(n_blocks)
+    ]
+    for copy in fetches:
+        copy.start()
+    lane = lax.broadcasted_iota(jnp.int32, (6, 128), 1)
+    sub = lax.broadcasted_iota(jnp.int32, (6, 128), 0)
+    sm_ref[...] = jnp.zeros_like(sm_ref)
+    for copy in smalls:
+        copy.wait()
+    for b in range(6):
+        sm_ref[b : b + 1, 0:EP] = pa_ref[b]
+    heads = sm_ref[0:6, :]
+    rows = jnp.where(lane == sub + EP, f32(1.0), f32(0.0))
+    steps = [tr_ref[c, :, 0, :] for c in range(6)]
+    for i in range(EP - 1, -1, -1):
+        wt_ref[:, i, :] = rows
+        terms = [steps[c][:, i : i + 1] * rows[c : c + 1, :] for c in range(6)]
+        new = ((terms[0] + terms[1]) + (terms[2] + terms[3])) + (terms[4] + terms[5])
+        rows = jnp.where(lane == i, heads, new)
+    sm_ref[0:6, :] = rows
+    sm_ref[6:7, 0:EP] = ob_ref[...]
+    lane1 = lax.broadcasted_iota(jnp.int32, (1, 128), 1)
+    sm_ref[7:8, :] = jnp.where((lane1 < EP) & (lane1 < cnt_ref[0, 0]), f32(1.0), f32(0.0))
+    weights = jnp.transpose(wt_ref[...].reshape(6 * EP, 128))[0:ROWS, :].astype(bf16)
+    small = jnp.concatenate([sm_ref[b : b + 1, :] for b in range(8)] + [jnp.zeros((1, 128), f32)], axis=1)
+    high = rounded(small)
+    row = lax.broadcasted_iota(jnp.int32, (8, BLK), 0)
+    tail = jnp.where(row == 6, high, jnp.where(row == 7, small - high, f32(0.0)))
+    for b in range(n_blocks):
+        fetches[b].wait()
+        local = jnp.dot(weights, fbuf[b].reshape(6 * EP, BLK), preferred_element_type=f32)
+        packed = jnp.concatenate([local[0:EP, :], local[EP:ROWS, :] + tail], axis=0).astype(bf16)
+        for h in range(2):
+            out_ref[b // 2 * 4 + 2 * h + b % 2] = packed
 
 
 def pack(counts, transition, partials, observed, forcing):
     n_blocks = forcing.shape[2] // BLK
-    hbm = pl.BlockSpec(memory_space=pl.ANY)
+    hbm = pl.BlockSpec(memory_space=pltpu.MemorySpace.HBM)
     return pl.pallas_call(
         pack_kernel,
-        grid=(n_blocks,),
-        out_shape=jax.ShapeDtypeStruct((n_blocks // 2, 2, 2, ROWS, BLK), bf16),
+        out_shape=jax.ShapeDtypeStruct((2 * n_blocks, ROWS, BLK), bf16),
         in_specs=[pl.BlockSpec(memory_space=pltpu.SMEM), hbm, hbm, hbm, hbm],
-        out_specs=pl.BlockSpec((1, 2, 1, ROWS, BLK), lambda j: (j // 2, 0, j % 2, 0, 0)),
+        out_specs=pl.BlockSpec(memory_space=pltpu.VMEM),
         scratch_shapes=[
             pltpu.VMEM((6, 6, 1, EP), f32),
             pltpu.VMEM((6, 1, EP), f32),
             pltpu.VMEM((1, EP), f32),
             pltpu.VMEM((n_blocks, 6, EP, BLK), bf16),
             pltpu.VMEM((6, EP, 128), f32),
-            pltpu.VMEM((ROWS, 6 * EP), bf16),
-            pltpu.VMEM((ROWS, BLK), f32),
             pltpu.VMEM((8, 128), f32),
             pltpu.SemaphoreType.DMA((n_blocks,)),
             pltpu.SemaphoreType.DMA((3,)),
         ],
-        compiler_params=pltpu.CompilerParams(vmem_limit_bytes=58 << 20),
+        compiler_params=pltpu.CompilerParams(vmem_limit_bytes=32 << 20),
         name="pack_rows",
-    )(counts, transition, partials, observed, forcing).reshape(2 * n_blocks, ROWS, BLK)
-
-
-def normal_kernel(place_ref, r_ref, keep_ref, send_ref, te_ref, tt_ref, in_ref, y_ref, n_ref, x_ref, l_ref, g_ref, rr_ref):
-    half = place_ref[0]
-    core = place_ref[1]
-    turn = place_ref[2]
+    )(counts, *[pltpu.with_memory_space_constraint(x, pltpu.MemorySpace.HBM) for x in (transition, partials, observed, forcing)])
+
+
+def normal_kernel(r_ref, keep_ref, send_ref, te_ref, tt_ref, in_ref, y_ref, n_ref, x_ref, l_ref, g_ref, rr_ref):
+    shard = lax.axis_index("tm")
+    half = lax.div(lax.rem(shard, 4), 2)
+    turn = lax.div(shard, 4)
+    core = lax.rem(lax.axis_index("arc"), 2)
     rows_of = [r_ref[t, 32:40, :].astype(f32) for t in range(TS)]
     for t in range(TS):
         small = rows_of[t][6:7, :] + rows_of[t][7:8, :]
@@ -217,14 +207,14 @@
             send_ref[slot] = block.astype(bf16)
 
 
-def normals(place, received):
+def normals(received):
     return pl.pallas_call(
         normal_kernel,
         out_shape=(
             jax.ShapeDtypeStruct((4, OUT_ROWS, BLK), f32),
             jax.ShapeDtypeStruct((4, OUT_ROWS, BLK), bf16),
         ),
-        in_specs=[pl.BlockSpec(memory_space=pltpu.SMEM), pl.BlockSpec(memory_space=pltpu.VMEM)],
+        in_specs=[pl.BlockSpec(memory_space=pltpu.VMEM)],
         out_specs=(pl.BlockSpec(memory_space=pltpu.VMEM), pl.BlockSpec(memory_space=pltpu.VMEM)),
         scratch_shapes=[
             pltpu.VMEM((128, 128), f32),
@@ -239,7 +229,7 @@
         ],
         compiler_params=pltpu.CompilerParams(vmem_limit_bytes=40 << 20),
         name="normal_rows",
-    )(place, received)
+    )(received)
 
 
 def local(transition, forcing, partials, observed, counts):
@@ -251,9 +241,7 @@
         jnp.transpose(forcing[0], (1, 0, 2)),
     )
     received = lax.all_to_all(packed, "tm", split_axis=0, concat_axis=0, tiled=True)
-    arc, tm = lax.axis_index("arc"), lax.axis_index("tm")
-    place = jnp.stack([tm % 4 // 2, arc % 2, tm // 4]).astype(jnp.int32)
-    keep, send = normals(place, received)
+    keep, send = normals(received)
     arcs, shards = lax.axis_size("arc"), lax.axis_size("tm")
     other_core = [(a * shards + t, (a ^ 1) * shards + t) for a in range(arcs) for t in range(shards)]
     arrived = lax.ppermute(send, ("arc", "tm"), other_core)

time: 81.7 us -> 77.2 us (0.945)
  blocking collectives: 17.2 us -> 43.6 us
  waiting for transfers between devices: 32.3 us -> 11.3 us
  starting transfers between devices: 10.3 us -> 3.16 us
  Pallas kernels: 18.3 us -> 15.6 us
    all_to_all x0 -> x1, blocking collectives: none -> 26.4 us  [local(): lax.all_to_all(packed, 'tm', split_axis=0, concat_axis=0, tiled=True)]
    all_to_all x1 -> x0, waiting for transfers between devices: 21 us -> none  [local(): lax.all_to_all(packed, 'tm', split_axis=0, concat_axis=0, tiled=True)]
    all_to_all x1 -> x0, starting transfers between devices: 7.18 us -> none  [local(): lax.all_to_all(packed, 'tm', split_axis=0, concat_axis=0, tiled=True)]
    pallas_call x1, Pallas kernels: 7.02 us -> 4.89 us  [pack(): pl.pallas_call(pack_kernel, out_shape=jax.ShapeDtypeStruct((2 * n_blocks,...]
  transfers between devices with their start and end apart: 3 -> 2, of which waited for: 3 -> 2; matrix products, arithmetic and copies ran while one was open for 0% -> 0% of each run, Pallas kernels for 0% -> 0%
where the time goes in v3:
time: 77.2 us; the launch traced here: 76.5 us
  blocking collectives  43.6 us (56%)
  Pallas kernels  15.6 us (20%)
  waiting for transfers between devices  11.3 us (15%)
  starting transfers between devices  3.16 us (4%)
  between operations  1.32 us (2%)
  local copies, waits for them, and re-layouts  1.26 us (2%)
    all_to_all x1, blocking collectives, local(): lax.all_to_all(packed, 'tm', split_axis=0, concat_axis=0, tiled=True)  26.4 us
    all_to_all x1, blocking collectives, local(): lax.all_to_all(pair_sum, 'arc', split_axis=0, concat_axis=0, tiled=True,...  17.2 us
    pallas_call x1, Pallas kernels, normals(): pl.pallas_call(normal_kernel, out_shape=(jax.ShapeDtypeStruct((4, OUT_ROW...  10.7 us
    ppermute x1, waiting for transfers between devices, local(): final = lax.ppermute(mine, ('arc', 'tm'), to_owner).astype(f32)  9.1 us
    pallas_call x1, Pallas kernels, pack(): pl.pallas_call(pack_kernel, out_shape=jax.ShapeDtypeStruct((2 * n_blocks,...  4.89 us
    ppermute x1, starting transfers between devices, local(): final = lax.ppermute(mine, ('arc', 'tm'), to_owner).astype(f32)  3.08 us
    ppermute x1, waiting for transfers between devices, local(): arrived = lax.ppermute(send, ('arc', 'tm'), other_core)  2.2 us
  transfers between devices with their start and end apart: 2, of which 2 were waited for; matrix products, arithmetic and copies ran while one was open for 0% of the time, Pallas kernels for 0%

profile of v3, /device:TPU:24, one launch (start us, length us, event | category | flops | bytes accessed | tf_op | source)
XLA Modules:
  0.0 76.5 jit_solution(12667646530988966105)
XLA Ops:
  1.3 4.9 %pack_rows.1 = bf16[16,40,1152]{2,1,0:T(8,128)(2,1)S(1)} custom-call(s32[1,1]{1,0:T(1,128)S(6)} %copy.7.cnt_ref, f32[6,6,1,32]{3,2,1,0:T(1,128)} %bitcast.8, f32[6,1,32]{2,1,0:T(1,128)} %bitcast.9, f32[1,32]{1,0:T(1,128)} %ob_hbm.1, bf16[6,32,9216]{2,1,0:T(8,128)(2,1)} %bitcast.7), custom_call_target="tpu_custom_call" | custom-call | tf_op jit(solution)/shard_map/pack_rows/pallas_call | solution.py:75
  6.2 26.4 %all_to_all.10.r_ref = bf16[16,40,1152]{2,1,0:T(8,128)(2,1)S(1)} all-to-all(bf16[16,40,1152]{2,1,0:T(8,128)(2,1)S(1)} %pack_rows.1), channel_id=1, replica_groups=mesh['arc'=8,'tm'=16] {'tm'}, dimensions={0} | all-to-all | bytes 2949120 | tf_op jit(solution)/shard_map/all_to_all | solution.py:243
  32.6 10.7 %normal_rows.1 = (f32[4,80,1152]{2,1,0:T(8,128)S(1)}, bf16[4,80,1152]{2,1,0:T(8,128)(2,1)S(1)}) custom-call(bf16[16,40,1152]{2,1,0:T(8,128)(2,1)S(1)} %all_to_all.10.r_ref), custom_call_target="tpu_custom_call" | custom-call | tf_op jit(solution)/shard_map/normal_rows/pallas_call | solution.py:211
  43.3 0.1 collective-permute-start
  43.4 2.2 %collective-permute-done = bf16[4,80,1152]{2,1,0:T(8,128)(2,1)S(1)} collective-permute-done((bf16[4,80,1152]{2,1,0:T(8,128)(2,1)S(1)}, bf16[4,80,1152]{2,1,0:T(8,128)(2,1)S(1)}, u32[]{:S(2)}, u32[]{:S(2)}) %collective-permute-start) | collective-permute-done | bytes 737312 | tf_op jit(solution)/shard_map/ppermute | solution.py:247
  45.6 0.2 add_convert_fusion
  45.8 17.2 %all_to_all.11 = bf16[4,80,1152]{2,1,0:T(8,128)(2,1)S(1)} all-to-all(bf16[4,80,1152]{2,1,0:T(8,128)(2,1)S(1)} %add_convert_fusion), channel_id=1, replica_groups={{0,32,64,96},{16,48,80,112},{1,33,65,97},{17,49,81,113},{2,34,66,98},{1..., dimensions={0} | all-to-all | bytes 1474560 | tf_op jit(solution)/shard_map/all_to_all | solution.py:250
  62.9 0.1 reduce_sum.12
  63.1 3.1 %collective-permute-start.1 = (bf16[80,1152]{1,0:T(8,128)(2,1)S(1)}, bf16[80,1152]{1,0:T(8,128)(2,1)S(1)}, u32[]{:S(2)}, u32[]{:S(2)}) collective-permute-start(bf16[80,1152]{1,0:T(8,128)(2,1)S(1)} %reduce_sum.12), channel_id=1, source_target_pairs={{0,0},{1,16},{2,2},{3,18},{4,36},{5,52},{6,38},{7,54},{8,72},{9,88... | collective-permute-start | bytes 552968 | tf_op jit(solution)/shard_map/ppermute | solution.py:257
  66.2 9.1 %collective-permute-done.1 = bf16[80,1152]{1,0:T(8,128)(2,1)S(1)} collective-permute-done((bf16[80,1152]{1,0:T(8,128)(2,1)S(1)}, bf16[80,1152]{1,0:T(8,128)(2,1)S(1)}, u32[]{:S(2)}, u32[]{:S(2)}) %collective-permute-start.1) | collective-permute-done | bytes 184352 | tf_op jit(solution)/shard_map/ppermute | solution.py:257
  75.3 0.5 slice_bitcast_fusion
  75.8 0.7 slice.8
  (1 shorter events, 0.0 us)
Async XLA Ops:
  43.3 2.3 %collective-permute-start = (bf16[4,80,1152]{2,1,0:T(8,128)(2,1)S(1)}, bf16[4,80,1152]{2,1,0:T(8,128)(2,1)S(1)}, u32[]{:S(2)}, u32[]{:S(2)}) collective-permute-start(bf16[4,80,1152]{2,1,0:T(8,128)(2,1)S(1)} %get-tuple-element.5), channel_id=1, source_target_pairs={{0,16},{1,17},{2,18},{3,19},{4,20},{5,21},{6,22},{7,23},{8,24},{9,... | collective-permute-start | bytes 2211848 | tf_op jit(solution)/shard_map/ppermute | solution.py:247
  63.1 12.2 %collective-permute-start.1 = (bf16[80,1152]{1,0:T(8,128)(2,1)S(1)}, bf16[80,1152]{1,0:T(8,128)(2,1)S(1)}, u32[]{:S(2)}, u32[]{:S(2)}) collective-permute-start(bf16[80,1152]{1,0:T(8,128)(2,1)S(1)} %reduce_sum.12), channel_id=1, source_target_pairs={{0,0},{1,16},{2,2},{3,18},{4,36},{5,52},{6,38},{7,54},{8,72},{9,88... | collective-permute-start | bytes 552968 | tf_op jit(solution)/shard_map/ppermute | solution.py:257

commit v4 on v3

--- a/solution.py
+++ b/solution.py
@@ -92,85 +92,91 @@
     )(counts, *[pltpu.with_memory_space_constraint(x, pltpu.MemorySpace.HBM) for x in (transition, partials, observed, forcing)])
 
 
-def normal_kernel(r_ref, keep_ref, send_ref, te_ref, tt_ref, in_ref, y_ref, n_ref, x_ref, l_ref, g_ref, rr_ref):
+def split(x):
+    high = x.astype(bf16)
+    return high, (x - high.astype(f32)).astype(bf16)
+
+
+def normal_kernel(r_ref, keep_ref, send_ref, te_ref, in_ref, lead_ref, y_ref, x_ref, l_ref, g_ref, rr_ref):
     shard = lax.axis_index("tm")
     half = lax.div(lax.rem(shard, 4), 2)
     turn = lax.div(shard, 4)
     core = lax.rem(lax.axis_index("arc"), 2)
-    rows_of = [r_ref[t, 32:40, :].astype(f32) for t in range(TS)]
-    for t in range(TS):
-        small = rows_of[t][6:7, :] + rows_of[t][7:8, :]
+    dims = (((0,), (0,)), ((), ()))
+    tails = [r_ref[t, 32:40, :].astype(f32) for t in range(TS)]
+    for t in range(TS):
+        small = tails[t][6:7, :] + tails[t][7:8, :]
         for b in range(8):
             te_ref[8 * t + b : 8 * t + b + 1, :] = small[:, 128 * b : 128 * b + 128]
-    turned = jnp.transpose(te_ref[...])[0:40, :]
-    for t in range(TS):
-        tt_ref[t] = turned if t == 0 else pltpu.roll(turned, 128 - 8 * t, 1)
+    turned = jnp.transpose(te_ref[...])
 
     sub = lax.broadcasted_iota(jnp.int32, (8, BLK), 0)
-    subw = lax.broadcasted_iota(jnp.int32, (8, WIDE), 0)
-    lanew = lax.broadcasted_iota(jnp.int32, (8, WIDE), 1)
-    state = jnp.where((lanew == subw + BLK) & (subw < 6), f32(1.0), f32(0.0))
-    for t in range(TS):
-        in_ref[t] = state
+    sub_aug = lax.broadcasted_iota(jnp.int32, (8, AUG), 0)
+    lane_aug = lax.broadcasted_iota(jnp.int32, (8, AUG), 1)
+    unit = jnp.where((sub_aug == 6) & (lane_aug == 6), f32(1.0), f32(0.0))
+    eye = jnp.where((lane_aug == sub_aug) & (sub_aug < 6), f32(1.0), f32(0.0))
+    state = jnp.concatenate([jnp.zeros((8, BLK), f32), eye + unit], axis=1)
+    for t in range(TS):
+        in_ref[8 * t : 8 * t + 8, :] = state
         if t == TS - 1:
             break
-        both = jnp.where(sub < 6, rows_of[t], f32(0.0))
-        new = jnp.concatenate([both, jnp.zeros((8, AUG), f32)], axis=1)
-        for b in range(6):
-            new = new + tt_ref[t, 32:40, b : b + 1] * state[b : b + 1, :]
-        state = new
-
-    lane_aug = lax.broadcasted_iota(jnp.int32, (EP, AUG), 1)
-
-    def rows_step(t, carry):
-        coef = tt_ref[t, 0:EP, :]
-        active = coef[:, 7:8] > f32(0.5)
-        base = jnp.concatenate(
-            [r_ref[t, 0:EP, :].astype(f32), jnp.where(lane_aug == 6, coef[:, 6:7], f32(0.0))], axis=1
-        )
-        for b in range(6):
-            base = base + coef[:, b : b + 1] * in_ref[t, b : b + 1, :]
-        y_ref[pl.ds(pl.multiple_of(t * EP, EP), EP), :] = jnp.where(active, base, f32(0.0))
-        return carry
-
-    lax.fori_loop(0, TS, rows_step, 0)
-
-    aug = y_ref[:, BLK:WIDE]
-    lane_all = lax.broadcasted_iota(jnp.int32, aug.shape, 1)
-    states = jnp.where(lane_all < 6, aug, f32(0.0))
-    high = states.astype(bf16)
-    low = (states - high.astype(f32)).astype(bf16)
-    low_aug = (aug - rounded(aug)).astype(bf16)
-    dims = (((0,), (0,)), ((), ()))
-    whole = y_ref[...].astype(bf16)
-    right = jnp.concatenate([whole, low_aug], axis=1)
-    n_high = lax.dot_general(high, right, dims, preferred_element_type=f32)[0:8]
-    n_low = lax.dot_general(low, right, dims, preferred_element_type=f32)[0:8]
-    total = n_high + n_low
-    augmented = total[:, BLK:WIDE] + total[:, WIDE:]
-    eye = jnp.where(
-        (lax.broadcasted_iota(jnp.int32, (8, AUG), 1) == lax.broadcasted_iota(jnp.int32, (8, AUG), 0)), f32(1.0), f32(0.0)
-    )
-    system = jnp.concatenate([total[:, 0:BLK], augmented + eye], axis=1)
+        new = jnp.concatenate([jnp.where(sub < 6, tails[t], f32(0.0)), unit], axis=1)
+        terms = [turned[32:40, 8 * t + b : 8 * t + b + 1] * state[b : b + 1, :] for b in range(6)]
+        state = new + (((terms[0] + terms[1]) + (terms[2] + terms[3])) + (terms[4] + terms[5]))
+
+    lane = lax.broadcasted_iota(jnp.int32, (EP, AUG), 1)
+    for t in range(TS):
+        active = turned[0:EP, 8 * t + 7 : 8 * t + 8] > f32(0.5)
+        mine = (lane >= 8 * t) & (lane < 8 * t + 7) & active
+        high, low = split(jnp.where(mine, turned[0:EP, :], f32(0.0)))
+        lead_ref[EP * t : EP * t + EP, 0:AUG] = high
+        lead_ref[EP * t : EP * t + EP, AUG : 2 * AUG] = low
+        lead_ref[EP * t : EP * t + EP, 2 * AUG : 3 * AUG] = high
+
+    maps = in_ref[:, BLK:WIDE]
+    maps_high, maps_low = split(maps)
+    states = jnp.dot(
+        lead_ref[...], jnp.concatenate([maps_high, maps_high, maps_low], axis=0), preferred_element_type=f32
+    )
+    states_high, states_low = split(states)
+    left = (states_high.astype(f32) + pltpu.roll(states_low.astype(f32), 8, 1)).astype(bf16)
+    rows = jnp.concatenate([r_ref[t, 0:EP, :] for t in range(TS)], axis=0)
+    from_local = lax.dot_general(left, rows, dims, preferred_element_type=f32)
+    right = jnp.concatenate([states_high, states_low, lead_ref[:, 0 : 2 * AUG]], axis=1)
+    from_small = lax.dot_general(left, right, dims, preferred_element_type=f32)
+    from_small = from_small[0:8, :] + from_small[8:16, :]
+    augmented = from_small[:, 0:AUG] + from_small[:, AUG : 2 * AUG]
+    through = from_small[:, 2 * AUG : 3 * AUG] + from_small[:, 3 * AUG : 4 * AUG]
+    through_high, through_low = split(through)
+    sums_high, sums_low = split(in_ref[:, 0:BLK])
+    from_sums = jnp.dot(
+        jnp.concatenate([through_high, through_low, through_high], axis=1),
+        jnp.concatenate([sums_high, sums_high, sums_low], axis=0),
+        preferred_element_type=f32,
+    )
+    system = jnp.concatenate([from_local[0:8, :] + from_local[8:16, :] + from_sums, augmented + eye], axis=1)
     row_id = lax.broadcasted_iota(jnp.int32, (8, WIDE), 0)
     for p in range(6):
         column = system[:, BLK + p : BLK + p + 1]
-        pivot = system[p : p + 1, :] / system[p : p + 1, BLK + p : BLK + p + 1]
+        pivot = system[p : p + 1, :] * (f32(1.0) / system[p : p + 1, BLK + p : BLK + p + 1])
         system = jnp.where(row_id == p, pivot, system - column * pivot)
-    n_ref[...] = system
-
-    def reduce_step(t, carry):
-        at = pl.ds(pl.multiple_of(t * EP, EP), EP)
-        rows = y_ref[at, :]
-        coef = rows[:, BLK:WIDE]
-        for b in range(6):
-            rows = rows - coef[:, b : b + 1] * n_ref[b : b + 1, :]
-        x_ref[at, :] = rows[:, 0:BLK].astype(bf16)
-        tail = jnp.where(lane_aug == 6, rows[:, BLK:WIDE], f32(0.0))
+
+    for t in range(TS):
+        at = slice(8 * t, 8 * t + 8)
+        terms = [in_ref[at, BLK + c : BLK + c + 1] * system[c : c + 1, :] for c in range(6)]
+        in_ref[at, :] = in_ref[at, :] - (((terms[0] + terms[1]) + (terms[2] + terms[3])) + (terms[4] + terms[5]))
+    change_high, change_low = split(in_ref[...])
+    y_ref[...] = jnp.dot(
+        lead_ref[...], jnp.concatenate([change_high, change_high, change_low], axis=0), preferred_element_type=f32
+    )
+    lane_tail = lax.broadcasted_iota(jnp.int32, (EP, AUG), 1)
+    for t in range(TS):
+        at = slice(EP * t, EP * t + EP)
+        active = turned[0:EP, 8 * t + 7 : 8 * t + 8] > f32(0.5)
+        local = jnp.where(active, r_ref[t, 0:EP, :].astype(f32), f32(0.0))
+        x_ref[at, :] = (local + y_ref[at, 0:BLK]).astype(bf16)
+        tail = jnp.where(lane_tail == 6, y_ref[at, BLK:WIDE], f32(0.0))
         l_ref[at, HALF : HALF + 64] = pltpu.roll(tail, 122, 1)[:, 0:64].astype(bf16)
-        return carry
-
-    lax.fori_loop(0, TS, reduce_step, 0)
 
     for side in range(2):
 
@@ -217,11 +223,10 @@
         in_specs=[pl.BlockSpec(memory_space=pltpu.VMEM)],
         out_specs=(pl.BlockSpec(memory_space=pltpu.VMEM), pl.BlockSpec(memory_space=pltpu.VMEM)),
         scratch_shapes=[
-            pltpu.VMEM((128, 128), f32),
-            pltpu.VMEM((TS, 40, 128), f32),
-            pltpu.VMEM((TS, 8, WIDE), f32),
+            pltpu.VMEM((8 * TS, 128), f32),
+            pltpu.VMEM((8 * TS, WIDE), f32),
+            pltpu.VMEM((TS * EP, 3 * AUG), bf16),
             pltpu.VMEM((TS * EP, WIDE), f32),
-            pltpu.VMEM((8, WIDE), f32),
             pltpu.VMEM((TS * EP, BLK), bf16),
             pltpu.VMEM((TS * EP, HALF + 64), bf16),
             pltpu.VMEM((HALF + 64, BLK), f32),

time: 77.2 us -> 71.5 us (0.926)
  Pallas kernels: 15.6 us -> 9.96 us
    pallas_call x1, Pallas kernels: 10.7 us -> 5.07 us  [normals(): pl.pallas_call(normal_kernel, out_shape=(jax.ShapeDtypeStruct((4, OUT_ROW...]
where the time goes in v4:
time: 71.5 us; the launch traced here: 70.9 us
  blocking collectives  43.6 us (61%)
  waiting for transfers between devices  11.3 us (16%)
  Pallas kernels  9.96 us (14%)
  starting transfers between devices  3.16 us (4%)
  between operations  1.32 us (2%)
  local copies, waits for them, and re-layouts  1.26 us (2%)
    all_to_all x1, blocking collectives, local(): lax.all_to_all(packed, 'tm', split_axis=0, concat_axis=0, tiled=True)  26.4 us
    all_to_all x1, blocking collectives, local(): lax.all_to_all(pair_sum, 'arc', split_axis=0, concat_axis=0, tiled=True,...  17.2 us
    ppermute x1, waiting for transfers between devices, local(): final = lax.ppermute(mine, ('arc', 'tm'), to_owner).astype(f32)  9.1 us
    pallas_call x1, Pallas kernels, normals(): pl.pallas_call(normal_kernel, out_shape=(jax.ShapeDtypeStruct((4, OUT_ROW...  5.07 us
    pallas_call x1, Pallas kernels, pack(): pl.pallas_call(pack_kernel, out_shape=jax.ShapeDtypeStruct((2 * n_blocks,...  4.89 us
    ppermute x1, starting transfers between devices, local(): final = lax.ppermute(mine, ('arc', 'tm'), to_owner).astype(f32)  3.08 us
    ppermute x1, waiting for transfers between devices, local(): arrived = lax.ppermute(send, ('arc', 'tm'), other_core)  2.2 us
  transfers between devices with their start and end apart: 2, of which 2 were waited for; matrix products, arithmetic and copies ran while one was open for 0% of the time, Pallas kernels for 0%

profile of v4, /device:TPU:24, one launch (start us, length us, event | category | flops | bytes accessed | tf_op | source)
XLA Modules:
  0.0 70.9 jit_solution(10031587563464768921)
XLA Ops:
  1.3 4.9 %pack_rows.1 = bf16[16,40,1152]{2,1,0:T(8,128)(2,1)S(1)} custom-call(s32[1,1]{1,0:T(1,128)S(6)} %copy.7.cnt_ref, f32[6,6,1,32]{3,2,1,0:T(1,128)} %bitcast.8, f32[6,1,32]{2,1,0:T(1,128)} %bitcast.9, f32[1,32]{1,0:T(1,128)} %ob_hbm.1, bf16[6,32,9216]{2,1,0:T(8,128)(2,1)} %bitcast.7), custom_call_target="tpu_custom_call" | custom-call | tf_op jit(solution)/shard_map/pack_rows/pallas_call | solution.py:75
  6.2 26.4 %all_to_all.10.r_ref = bf16[16,40,1152]{2,1,0:T(8,128)(2,1)S(1)} all-to-all(bf16[16,40,1152]{2,1,0:T(8,128)(2,1)S(1)} %pack_rows.1), channel_id=1, replica_groups=mesh['arc'=8,'tm'=16] {'tm'}, dimensions={0} | all-to-all | bytes 2949120 | tf_op jit(solution)/shard_map/all_to_all | solution.py:248
  32.6 5.1 %normal_rows.1 = (f32[4,80,1152]{2,1,0:T(8,128)S(1)}, bf16[4,80,1152]{2,1,0:T(8,128)(2,1)S(1)}) custom-call(bf16[16,40,1152]{2,1,0:T(8,128)(2,1)S(1)} %all_to_all.10.r_ref), custom_call_target="tpu_custom_call" | custom-call | tf_op jit(solution)/shard_map/normal_rows/pallas_call | solution.py:217
  37.6 0.1 collective-permute-start
  37.7 2.2 %collective-permute-done = bf16[4,80,1152]{2,1,0:T(8,128)(2,1)S(1)} collective-permute-done((bf16[4,80,1152]{2,1,0:T(8,128)(2,1)S(1)}, bf16[4,80,1152]{2,1,0:T(8,128)(2,1)S(1)}, u32[]{:S(2)}, u32[]{:S(2)}) %collective-permute-start) | collective-permute-done | bytes 737312 | tf_op jit(solution)/shard_map/ppermute | solution.py:252
  39.9 0.2 add_convert_fusion
  40.1 17.2 %all_to_all.11 = bf16[4,80,1152]{2,1,0:T(8,128)(2,1)S(1)} all-to-all(bf16[4,80,1152]{2,1,0:T(8,128)(2,1)S(1)} %add_convert_fusion), channel_id=1, replica_groups={{0,32,64,96},{16,48,80,112},{1,33,65,97},{17,49,81,113},{2,34,66,98},{1..., dimensions={0} | all-to-all | bytes 1474560 | tf_op jit(solution)/shard_map/all_to_all | solution.py:255
  57.3 0.1 reduce_sum.12
  57.4 3.1 %collective-permute-start.1 = (bf16[80,1152]{1,0:T(8,128)(2,1)S(1)}, bf16[80,1152]{1,0:T(8,128)(2,1)S(1)}, u32[]{:S(2)}, u32[]{:S(2)}) collective-permute-start(bf16[80,1152]{1,0:T(8,128)(2,1)S(1)} %reduce_sum.12), channel_id=1, source_target_pairs={{0,0},{1,16},{2,2},{3,18},{4,36},{5,52},{6,38},{7,54},{8,72},{9,88... | collective-permute-start | bytes 552968 | tf_op jit(solution)/shard_map/ppermute | solution.py:262
  60.5 9.1 %collective-permute-done.1 = bf16[80,1152]{1,0:T(8,128)(2,1)S(1)} collective-permute-done((bf16[80,1152]{1,0:T(8,128)(2,1)S(1)}, bf16[80,1152]{1,0:T(8,128)(2,1)S(1)}, u32[]{:S(2)}, u32[]{:S(2)}) %collective-permute-start.1) | collective-permute-done | bytes 184352 | tf_op jit(solution)/shard_map/ppermute | solution.py:262
  69.6 0.5 slice_bitcast_fusion
  70.1 0.7 %slice.8 = f32[72,1152]{1,0:T(8,128)} slice(bf16[80,1152]{1,0:T(8,128)(2,1)S(1)} %collective-permute-done.1), slice={[0:72], [0:1152]} | slice | bytes 663552 | tf_op jit(solution)/shard_map/slice | solution.py:263
  (1 shorter events, 0.0 us)
Async XLA Ops:
  37.6 2.3 %collective-permute-start = (bf16[4,80,1152]{2,1,0:T(8,128)(2,1)S(1)}, bf16[4,80,1152]{2,1,0:T(8,128)(2,1)S(1)}, u32[]{:S(2)}, u32[]{:S(2)}) collective-permute-start(bf16[4,80,1152]{2,1,0:T(8,128)(2,1)S(1)} %get-tuple-element.5), channel_id=1, source_target_pairs={{0,16},{1,17},{2,18},{3,19},{4,20},{5,21},{6,22},{7,23},{8,24},{9,... | collective-permute-start | bytes 2211848 | tf_op jit(solution)/shard_map/ppermute | solution.py:252
  57.4 12.2 %collective-permute-start.1 = (bf16[80,1152]{1,0:T(8,128)(2,1)S(1)}, bf16[80,1152]{1,0:T(8,128)(2,1)S(1)}, u32[]{:S(2)}, u32[]{:S(2)}) collective-permute-start(bf16[80,1152]{1,0:T(8,128)(2,1)S(1)} %reduce_sum.12), channel_id=1, source_target_pairs={{0,0},{1,16},{2,2},{3,18},{4,36},{5,52},{6,38},{7,54},{8,72},{9,88... | collective-permute-start | bytes 552968 | tf_op jit(solution)/shard_map/ppermute | solution.py:262

commit v5 on v4

--- a/solution.py
+++ b/solution.py
@@ -25,16 +25,14 @@
 def pack_kernel(
     cnt_ref, tr_hbm, pa_hbm, ob_hbm, f_hbm, out_ref, tr_ref, pa_ref, ob_ref, fbuf, wt_ref, sm_ref, sems, small_sems
 ):
-    n_blocks = fbuf.shape[0]
+    n_blocks = fbuf.shape[2] // BLK
     smalls = [
         pltpu.make_async_copy(src, dst, small_sems.at[n])
         for n, (src, dst) in enumerate(((tr_hbm, tr_ref), (pa_hbm, pa_ref), (ob_hbm, ob_ref)))
     ]
     for copy in smalls:
         copy.start()
-    fetches = [
-        pltpu.make_async_copy(f_hbm.at[:, :, pl.ds(b * BLK, BLK)], fbuf.at[b], sems.at[b]) for b in range(n_blocks)
-    ]
+    fetches = [pltpu.make_async_copy(f_hbm, fbuf, sems.at[0])]
     for copy in fetches:
         copy.start()
     lane = lax.broadcasted_iota(jnp.int32, (6, 128), 1)
@@ -61,9 +59,10 @@
     high = rounded(small)
     row = lax.broadcasted_iota(jnp.int32, (8, BLK), 0)
     tail = jnp.where(row == 6, high, jnp.where(row == 7, small - high, f32(0.0)))
+    for copy in fetches:
+        copy.wait()
     for b in range(n_blocks):
-        fetches[b].wait()
-        local = jnp.dot(weights, fbuf[b].reshape(6 * EP, BLK), preferred_element_type=f32)
+        local = jnp.dot(weights, fbuf[:, :, b * BLK : (b + 1) * BLK].reshape(6 * EP, BLK), preferred_element_type=f32)
         packed = jnp.concatenate([local[0:EP, :], local[EP:ROWS, :] + tail], axis=0).astype(bf16)
         for h in range(2):
             out_ref[b // 2 * 4 + 2 * h + b % 2] = packed
@@ -81,10 +80,10 @@
             pltpu.VMEM((6, 6, 1, EP), f32),
             pltpu.VMEM((6, 1, EP), f32),
             pltpu.VMEM((1, EP), f32),
-            pltpu.VMEM((n_blocks, 6, EP, BLK), bf16),
+            pltpu.VMEM((6, EP, n_blocks * BLK), bf16),
             pltpu.VMEM((6, EP, 128), f32),
             pltpu.VMEM((8, 128), f32),
-            pltpu.SemaphoreType.DMA((n_blocks,)),
+            pltpu.SemaphoreType.DMA((1,)),
             pltpu.SemaphoreType.DMA((3,)),
         ],
         compiler_params=pltpu.CompilerParams(vmem_limit_bytes=32 << 20),
@@ -100,7 +99,7 @@
 def normal_kernel(r_ref, keep_ref, send_ref, te_ref, in_ref, lead_ref, y_ref, x_ref, l_ref, g_ref, rr_ref):
     shard = lax.axis_index("tm")
     half = lax.div(lax.rem(shard, 4), 2)
-    turn = lax.div(shard, 4)
+    turn = 2 * lax.div(shard, 4) + 2
     core = lax.rem(lax.axis_index("arc"), 2)
     dims = (((0,), (0,)), ((), ()))
     tails = [r_ref[t, 32:40, :].astype(f32) for t in range(TS)]
@@ -199,7 +198,7 @@
                 rr_ref[:, 2 * SLICE * q : 2 * SLICE * (q + 1)] = g_ref[HALF : HALF + 8, first : first + 2 * SLICE]
 
     for s in range(8):
-        slot, parity = lax.rem(s // 2 + 4 - turn, 4), s % 2
+        slot, parity = lax.rem(turn + 4 - s // 2, 4), s % 2
         beside = rr_ref[:, SLICE * s : SLICE * (s + 1)]
         extra = jnp.concatenate([beside, jnp.zeros((8, BLK - SLICE), f32)], axis=1)
         block = jnp.concatenate([g_ref[SLICE * s : SLICE * (s + 1), :], extra], axis=0)
@@ -258,7 +257,7 @@
     for a in range(arcs):
         for t in range(shards):
             z, c, y, h, odd = a // 2, a % 2, t // 4, t % 4 // 2, t % 2
-            to_owner.append((a * shards + t, (2 * y + odd) * shards + (y + z) % 4 * 4 + 2 * h + c))
+            to_owner.append((a * shards + t, (2 * y + odd) * shards + (2 * y + 2 - z) % 4 * 4 + 2 * h + c))
     final = lax.ppermute(mine, ("arc", "tm"), to_owner).astype(f32)
     return final[0:SLICE, :], final[SLICE, 0:SLICE]
 

time: 71.5 us -> 67.7 us (0.947)
  Pallas kernels: 9.96 us -> 8.02 us
  waiting for transfers between devices: 11.3 us -> 9.51 us
    pallas_call x1, Pallas kernels: 4.89 us -> 2.94 us  [pack(): pl.pallas_call(pack_kernel, out_shape=jax.ShapeDtypeStruct((2 * n_blocks,...]
    ppermute x1, waiting for transfers between devices: 9.1 us -> 7.31 us  [local(): final = lax.ppermute(mine, ('arc', 'tm'), to_owner).astype(f32)]
where the time goes in v5:
time: 67.7 us; the launch traced here: 67.1 us
  blocking collectives  43.6 us (64%)
  waiting for transfers between devices  9.51 us (14%)
  Pallas kernels  8.02 us (12%)
  starting transfers between devices  3.14 us (5%)
  between operations  1.31 us (2%)
  local copies, waits for them, and re-layouts  1.26 us (2%)
    all_to_all x1, blocking collectives, local(): lax.all_to_all(packed, 'tm', split_axis=0, concat_axis=0, tiled=True)  26.4 us
    all_to_all x1, blocking collectives, local(): lax.all_to_all(pair_sum, 'arc', split_axis=0, concat_axis=0, tiled=True,...  17.2 us
    ppermute x1, waiting for transfers between devices, local(): final = lax.ppermute(mine, ('arc', 'tm'), to_owner).astype(f32)  7.31 us
    pallas_call x1, Pallas kernels, normals(): pl.pallas_call(normal_kernel, out_shape=(jax.ShapeDtypeStruct((4, OUT_ROW...  5.08 us
    ppermute x1, starting transfers between devices, local(): final = lax.ppermute(mine, ('arc', 'tm'), to_owner).astype(f32)  3.05 us
    pallas_call x1, Pallas kernels, pack(): pl.pallas_call(pack_kernel, out_shape=jax.ShapeDtypeStruct((2 * n_blocks,...  2.94 us
    ppermute x1, waiting for transfers between devices, local(): arrived = lax.ppermute(send, ('arc', 'tm'), other_core)  2.2 us
  transfers between devices with their start and end apart: 2, of which 2 were waited for; matrix products, arithmetic and copies ran while one was open for 0% of the time, Pallas kernels for 0%

profile of v5, /device:TPU:24, one launch (start us, length us, event | category | flops | bytes accessed | tf_op | source)
XLA Modules:
  0.0 67.1 jit_solution(10622319966649934673)
XLA Ops:
  1.3 2.9 %pack_rows.1 = bf16[16,40,1152]{2,1,0:T(8,128)(2,1)S(1)} custom-call(s32[1,1]{1,0:T(1,128)S(6)} %copy.7.cnt_ref, f32[6,6,1,32]{3,2,1,0:T(1,128)} %bitcast.8, f32[6,1,32]{2,1,0:T(1,128)} %bitcast.9, f32[1,32]{1,0:T(1,128)} %ob_hbm.1, bf16[6,32,9216]{2,1,0:T(8,128)(2,1)} %bitcast.7), custom_call_target="tpu_custom_call" | custom-call | tf_op jit(solution)/shard_map/pack_rows/pallas_call | solution.py:74
  4.2 26.4 %all_to_all.10.r_ref = bf16[16,40,1152]{2,1,0:T(8,128)(2,1)S(1)} all-to-all(bf16[16,40,1152]{2,1,0:T(8,128)(2,1)S(1)} %pack_rows.1), channel_id=1, replica_groups=mesh['arc'=8,'tm'=16] {'tm'}, dimensions={0} | all-to-all | bytes 2949120 | tf_op jit(solution)/shard_map/all_to_all | solution.py:247
  30.6 5.1 %normal_rows.1 = (f32[4,80,1152]{2,1,0:T(8,128)S(1)}, bf16[4,80,1152]{2,1,0:T(8,128)(2,1)S(1)}) custom-call(bf16[16,40,1152]{2,1,0:T(8,128)(2,1)S(1)} %all_to_all.10.r_ref), custom_call_target="tpu_custom_call" | custom-call | tf_op jit(solution)/shard_map/normal_rows/pallas_call | solution.py:216
  35.7 0.1 collective-permute-start
  35.8 2.2 %collective-permute-done = bf16[4,80,1152]{2,1,0:T(8,128)(2,1)S(1)} collective-permute-done((bf16[4,80,1152]{2,1,0:T(8,128)(2,1)S(1)}, bf16[4,80,1152]{2,1,0:T(8,128)(2,1)S(1)}, u32[]{:S(2)}, u32[]{:S(2)}) %collective-permute-start) | collective-permute-done | bytes 737312 | tf_op jit(solution)/shard_map/ppermute | solution.py:251
  38.0 0.2 add_convert_fusion
  38.2 17.2 %all_to_all.11 = bf16[4,80,1152]{2,1,0:T(8,128)(2,1)S(1)} all-to-all(bf16[4,80,1152]{2,1,0:T(8,128)(2,1)S(1)} %add_convert_fusion), channel_id=1, replica_groups={{0,32,64,96},{16,48,80,112},{1,33,65,97},{17,49,81,113},{2,34,66,98},{1..., dimensions={0} | all-to-all | bytes 1474560 | tf_op jit(solution)/shard_map/all_to_all | solution.py:254
  55.3 0.1 reduce_sum.12
  55.5 3.1 %collective-permute-start.1 = (bf16[80,1152]{1,0:T(8,128)(2,1)S(1)}, bf16[80,1152]{1,0:T(8,128)(2,1)S(1)}, u32[]{:S(2)}, u32[]{:S(2)}) collective-permute-start(bf16[80,1152]{1,0:T(8,128)(2,1)S(1)} %reduce_sum.12), channel_id=1, source_target_pairs={{0,8},{1,24},{2,10},{3,26},{4,32},{5,48},{6,34},{7,50},{8,72},{9,8... | collective-permute-start | bytes 552968 | tf_op jit(solution)/shard_map/ppermute | solution.py:261
  58.5 7.3 %collective-permute-done.1 = bf16[80,1152]{1,0:T(8,128)(2,1)S(1)} collective-permute-done((bf16[80,1152]{1,0:T(8,128)(2,1)S(1)}, bf16[80,1152]{1,0:T(8,128)(2,1)S(1)}, u32[]{:S(2)}, u32[]{:S(2)}) %collective-permute-start.1) | collective-permute-done | bytes 184352 | tf_op jit(solution)/shard_map/ppermute | solution.py:261
  65.8 0.5 slice_bitcast_fusion
  66.4 0.7 %slice.8 = f32[72,1152]{1,0:T(8,128)} slice(bf16[80,1152]{1,0:T(8,128)(2,1)S(1)} %collective-permute-done.1), slice={[0:72], [0:1152]} | slice | bytes 663552 | tf_op jit(solution)/shard_map/slice | solution.py:262
  (1 shorter events, 0.0 us)
Async XLA Ops:
  35.7 2.3 %collective-permute-start = (bf16[4,80,1152]{2,1,0:T(8,128)(2,1)S(1)}, bf16[4,80,1152]{2,1,0:T(8,128)(2,1)S(1)}, u32[]{:S(2)}, u32[]{:S(2)}) collective-permute-start(bf16[4,80,1152]{2,1,0:T(8,128)(2,1)S(1)} %get-tuple-element.5), channel_id=1, source_target_pairs={{0,16},{1,17},{2,18},{3,19},{4,20},{5,21},{6,22},{7,23},{8,24},{9,... | collective-permute-start | bytes 2211848 | tf_op jit(solution)/shard_map/ppermute | solution.py:251
  55.5 10.4 %collective-permute-start.1 = (bf16[80,1152]{1,0:T(8,128)(2,1)S(1)}, bf16[80,1152]{1,0:T(8,128)(2,1)S(1)}, u32[]{:S(2)}, u32[]{:S(2)}) collective-permute-start(bf16[80,1152]{1,0:T(8,128)(2,1)S(1)} %reduce_sum.12), channel_id=1, source_target_pairs={{0,8},{1,24},{2,10},{3,26},{4,32},{5,48},{6,34},{7,50},{8,72},{9,8... | collective-permute-start | bytes 552968 | tf_op jit(solution)/shard_map/ppermute | solution.py:261

commit v6 on v5

--- a/solution.py
+++ b/solution.py
@@ -23,7 +23,7 @@
 
 
 def pack_kernel(
-    cnt_ref, tr_hbm, pa_hbm, ob_hbm, f_hbm, out_ref, tr_ref, pa_ref, ob_ref, fbuf, wt_ref, sm_ref, sems, small_sems
+    cnt_ref, tr_hbm, pa_hbm, ob_hbm, f_hbm, out_ref, tr_ref, pa_ref, ob_ref, fbuf, one_ref, wt_ref, sm_ref, sems, small_sems
 ):
     n_blocks = fbuf.shape[2] // BLK
     smalls = [
@@ -32,25 +32,52 @@
     ]
     for copy in smalls:
         copy.start()
-    fetches = [pltpu.make_async_copy(f_hbm, fbuf, sems.at[0])]
+    middle = n_blocks // 2
+    parts = [pl.ds(0, middle * BLK), pl.ds(middle * BLK, (n_blocks - middle) * BLK)]
+    fetches = [pltpu.make_async_copy(f_hbm.at[:, :, p], fbuf.at[:, :, p], sems.at[n]) for n, p in enumerate(parts)]
     for copy in fetches:
         copy.start()
-    lane = lax.broadcasted_iota(jnp.int32, (6, 128), 1)
-    sub = lax.broadcasted_iota(jnp.int32, (6, 128), 0)
+    lane = lax.broadcasted_iota(jnp.int32, (8, 128), 1)
+    sub = lax.broadcasted_iota(jnp.int32, (8, 128), 0)
     sm_ref[...] = jnp.zeros_like(sm_ref)
+    one_ref[...] = jnp.zeros_like(one_ref)
     for copy in smalls:
         copy.wait()
     for b in range(6):
         sm_ref[b : b + 1, 0:EP] = pa_ref[b]
-    heads = sm_ref[0:6, :]
-    rows = jnp.where(lane == sub + EP, f32(1.0), f32(0.0))
-    steps = [tr_ref[c, :, 0, :] for c in range(6)]
-    for i in range(EP - 1, -1, -1):
-        wt_ref[:, i, :] = rows
-        terms = [steps[c][:, i : i + 1] * rows[c : c + 1, :] for c in range(6)]
-        new = ((terms[0] + terms[1]) + (terms[2] + terms[3])) + (terms[4] + terms[5])
-        rows = jnp.where(lane == i, heads, new)
-    sm_ref[0:6, :] = rows
+        one_ref[b, 0:6, 0:EP] = tr_ref[b, :, 0, :]
+    heads = sm_ref[...]
+
+    def total(terms):
+        return ((terms[0] + terms[1]) + (terms[2] + terms[3])) + (terms[4] + terms[5])
+
+    def applied(maps, vectors):
+        return total([maps[c] * vectors[c : c + 1, :] for c in range(6)])
+
+    def at(maps, epoch):
+        return [maps[c][:, epoch : epoch + 1] for c in range(6)]
+
+    one = [one_ref[c] for c in range(6)]
+    back = [[pltpu.roll(one[c], n, 1) for c in range(6)] for n in (1, 2, 3)]
+    two = [total([one[c][m : m + 1, :] * back[0][m] for m in range(6)]) for c in range(6)]
+    two_back = [pltpu.roll(two[c], 2, 1) for c in range(6)]
+    four = [total([two[c][m : m + 1, :] * two_back[m] for m in range(6)]) for c in range(6)]
+    heads_one = applied(back[0], heads)
+    heads_two = applied(back[1], heads_one)
+    heads_three = applied(back[2], heads_two)
+    phase = lane & 3
+    fresh = jnp.where(
+        phase == 3, heads_three, jnp.where(phase == 2, heads_two, jnp.where(phase == 1, heads_one, heads))
+    )
+    rows = jnp.where((lane == sub + EP) & (sub < 6), f32(1.0), f32(0.0))
+    for i in range(EP - 1, -1, -4):
+        first = jnp.where(lane == i, heads, applied(at(one, i), rows))
+        second = jnp.where(lane == i - 1, heads, jnp.where(lane == i, heads_one, applied(at(two, i), rows)))
+        third = jnp.where(lane == i - 2, heads, applied(at(one, i - 2), second))
+        for n, value in enumerate((rows, first, second, third)):
+            wt_ref[:, i - n, :] = value[0:6, :]
+        rows = jnp.where((lane >= i - 3) & (lane <= i), fresh, applied(at(four, i), rows))
+    sm_ref[0:6, :] = rows[0:6, :]
     sm_ref[6:7, 0:EP] = ob_ref[...]
     lane1 = lax.broadcasted_iota(jnp.int32, (1, 128), 1)
     sm_ref[7:8, :] = jnp.where((lane1 < EP) & (lane1 < cnt_ref[0, 0]), f32(1.0), f32(0.0))
@@ -59,9 +86,9 @@
     high = rounded(small)
     row = lax.broadcasted_iota(jnp.int32, (8, BLK), 0)
     tail = jnp.where(row == 6, high, jnp.where(row == 7, small - high, f32(0.0)))
-    for copy in fetches:
-        copy.wait()
     for b in range(n_blocks):
+        if b % middle == 0:
+            fetches[b // middle].wait()
         local = jnp.dot(weights, fbuf[:, :, b * BLK : (b + 1) * BLK].reshape(6 * EP, BLK), preferred_element_type=f32)
         packed = jnp.concatenate([local[0:EP, :], local[EP:ROWS, :] + tail], axis=0).astype(bf16)
         for h in range(2):
@@ -81,9 +108,10 @@
             pltpu.VMEM((6, 1, EP), f32),
             pltpu.VMEM((1, EP), f32),
             pltpu.VMEM((6, EP, n_blocks * BLK), bf16),
+            pltpu.VMEM((6, 8, 128), f32),
             pltpu.VMEM((6, EP, 128), f32),
             pltpu.VMEM((8, 128), f32),
-            pltpu.SemaphoreType.DMA((1,)),
+            pltpu.SemaphoreType.DMA((2,)),
             pltpu.SemaphoreType.DMA((3,)),
         ],
         compiler_params=pltpu.CompilerParams(vmem_limit_bytes=32 << 20),

time: 67.7 us -> 67.4 us (level)
  no operation moved by 1% of the time
where the time goes in v6:
time: 67.4 us; the launch traced here: 66.8 us
  blocking collectives  43.6 us (65%)
  waiting for transfers between devices  9.5 us (14%)
  Pallas kernels  7.72 us (11%)
  starting transfers between devices  3.14 us (5%)
  between operations  1.31 us (2%)
  local copies, waits for them, and re-layouts  1.26 us (2%)
    all_to_all x1, blocking collectives, local(): lax.all_to_all(packed, 'tm', split_axis=0, concat_axis=0, tiled=True)  26.4 us
    all_to_all x1, blocking collectives, local(): lax.all_to_all(pair_sum, 'arc', split_axis=0, concat_axis=0, tiled=True,...  17.2 us
    ppermute x1, waiting for transfers between devices, local(): final = lax.ppermute(mine, ('arc', 'tm'), to_owner).astype(f32)  7.3 us
    pallas_call x1, Pallas kernels, normals(): pl.pallas_call(normal_kernel, out_shape=(jax.ShapeDtypeStruct((4, OUT_ROW...  5.07 us
    ppermute x1, starting transfers between devices, local(): final = lax.ppermute(mine, ('arc', 'tm'), to_owner).astype(f32)  3.06 us
    pallas_call x1, Pallas kernels, pack(): pl.pallas_call(pack_kernel, out_shape=jax.ShapeDtypeStruct((2 * n_blocks,...  2.65 us
    ppermute x1, waiting for transfers between devices, local(): arrived = lax.ppermute(send, ('arc', 'tm'), other_core)  2.2 us
  transfers between devices with their start and end apart: 2, of which 2 were waited for; matrix products, arithmetic and copies ran while one was open for 0% of the time, Pallas kernels for 0%

profile of v6, /device:TPU:24, one launch (start us, length us, event | category | flops | bytes accessed | tf_op | source)
XLA Modules:
  0.0 66.8 jit_solution(12443817313699906051)
XLA Ops:
  1.3 2.6 %pack_rows.1 = bf16[16,40,1152]{2,1,0:T(8,128)(2,1)S(1)} custom-call(s32[1,1]{1,0:T(1,128)S(6)} %copy.7.cnt_ref, f32[6,6,1,32]{3,2,1,0:T(1,128)} %bitcast.8, f32[6,1,32]{2,1,0:T(1,128)} %bitcast.9, f32[1,32]{1,0:T(1,128)} %ob_hbm.1, bf16[6,32,9216]{2,1,0:T(8,128)(2,1)} %bitcast.7), custom_call_target="tpu_custom_call" | custom-call | tf_op jit(solution)/shard_map/pack_rows/pallas_call | solution.py:101
  3.9 26.4 %all_to_all.10.r_ref = bf16[16,40,1152]{2,1,0:T(8,128)(2,1)S(1)} all-to-all(bf16[16,40,1152]{2,1,0:T(8,128)(2,1)S(1)} %pack_rows.1), channel_id=1, replica_groups=mesh['arc'=8,'tm'=16] {'tm'}, dimensions={0} | all-to-all | bytes 2949120 | tf_op jit(solution)/shard_map/all_to_all | solution.py:275
  30.3 5.1 %normal_rows.1 = (f32[4,80,1152]{2,1,0:T(8,128)S(1)}, bf16[4,80,1152]{2,1,0:T(8,128)(2,1)S(1)}) custom-call(bf16[16,40,1152]{2,1,0:T(8,128)(2,1)S(1)} %all_to_all.10.r_ref), custom_call_target="tpu_custom_call" | custom-call | tf_op jit(solution)/shard_map/normal_rows/pallas_call | solution.py:244
  35.4 0.1 collective-permute-start
  35.5 2.2 %collective-permute-done = bf16[4,80,1152]{2,1,0:T(8,128)(2,1)S(1)} collective-permute-done((bf16[4,80,1152]{2,1,0:T(8,128)(2,1)S(1)}, bf16[4,80,1152]{2,1,0:T(8,128)(2,1)S(1)}, u32[]{:S(2)}, u32[]{:S(2)}) %collective-permute-start) | collective-permute-done | bytes 737312 | tf_op jit(solution)/shard_map/ppermute | solution.py:279
  37.7 0.2 add_convert_fusion
  37.9 17.2 %all_to_all.11 = bf16[4,80,1152]{2,1,0:T(8,128)(2,1)S(1)} all-to-all(bf16[4,80,1152]{2,1,0:T(8,128)(2,1)S(1)} %add_convert_fusion), channel_id=1, replica_groups={{0,32,64,96},{16,48,80,112},{1,33,65,97},{17,49,81,113},{2,34,66,98},{1..., dimensions={0} | all-to-all | bytes 1474560 | tf_op jit(solution)/shard_map/all_to_all | solution.py:282
  55.0 0.1 reduce_sum.12
  55.2 3.1 %collective-permute-start.1 = (bf16[80,1152]{1,0:T(8,128)(2,1)S(1)}, bf16[80,1152]{1,0:T(8,128)(2,1)S(1)}, u32[]{:S(2)}, u32[]{:S(2)}) collective-permute-start(bf16[80,1152]{1,0:T(8,128)(2,1)S(1)} %reduce_sum.12), channel_id=1, source_target_pairs={{0,8},{1,24},{2,10},{3,26},{4,32},{5,48},{6,34},{7,50},{8,72},{9,8... | collective-permute-start | bytes 552968 | tf_op jit(solution)/shard_map/ppermute | solution.py:289
  58.2 7.3 %collective-permute-done.1 = bf16[80,1152]{1,0:T(8,128)(2,1)S(1)} collective-permute-done((bf16[80,1152]{1,0:T(8,128)(2,1)S(1)}, bf16[80,1152]{1,0:T(8,128)(2,1)S(1)}, u32[]{:S(2)}, u32[]{:S(2)}) %collective-permute-start.1) | collective-permute-done | bytes 184352 | tf_op jit(solution)/shard_map/ppermute | solution.py:289
  65.5 0.5 slice_bitcast_fusion
  66.1 0.7 %slice.8 = f32[72,1152]{1,0:T(8,128)} slice(bf16[80,1152]{1,0:T(8,128)(2,1)S(1)} %collective-permute-done.1), slice={[0:72], [0:1152]} | slice | bytes 663552 | tf_op jit(solution)/shard_map/slice | solution.py:290
  (1 shorter events, 0.0 us)
Async XLA Ops:
  35.4 2.3 %collective-permute-start = (bf16[4,80,1152]{2,1,0:T(8,128)(2,1)S(1)}, bf16[4,80,1152]{2,1,0:T(8,128)(2,1)S(1)}, u32[]{:S(2)}, u32[]{:S(2)}) collective-permute-start(bf16[4,80,1152]{2,1,0:T(8,128)(2,1)S(1)} %get-tuple-element.5), channel_id=1, source_target_pairs={{0,16},{1,17},{2,18},{3,19},{4,20},{5,21},{6,22},{7,23},{8,24},{9,... | collective-permute-start | bytes 2211848 | tf_op jit(solution)/shard_map/ppermute | solution.py:279
  55.2 10.4 %collective-permute-start.1 = (bf16[80,1152]{1,0:T(8,128)(2,1)S(1)}, bf16[80,1152]{1,0:T(8,128)(2,1)S(1)}, u32[]{:S(2)}, u32[]{:S(2)}) collective-permute-start(bf16[80,1152]{1,0:T(8,128)(2,1)S(1)} %reduce_sum.12), channel_id=1, source_target_pairs={{0,8},{1,24},{2,10},{3,26},{4,32},{5,48},{6,34},{7,50},{8,72},{9,8... | collective-permute-start | bytes 552968 | tf_op jit(solution)/shard_map/ppermute | solution.py:289

commit v7 on v6

--- a/solution.py
+++ b/solution.py
@@ -10,7 +10,6 @@
 HALF = 576
 SLICE = 72
 ROWS = 40
-OUT_ROWS = 80
 TS = 16
 AUG = 128
 WIDE = BLK + AUG
@@ -124,7 +123,7 @@
     return high, (x - high.astype(f32)).astype(bf16)
 
 
-def normal_kernel(r_ref, keep_ref, send_ref, te_ref, in_ref, lead_ref, y_ref, x_ref, l_ref, g_ref, rr_ref):
+def normal_kernel(r_ref, keep_ref, send_ref, code_ref, te_ref, in_ref, lead_ref, y_ref, x_ref, l_ref, g_ref):
     shard = lax.axis_index("tm")
     half = lax.div(lax.rem(shard, 4), 2)
     turn = 2 * lax.div(shard, 4) + 2
@@ -201,9 +200,8 @@
         at = slice(EP * t, EP * t + EP)
         active = turned[0:EP, 8 * t + 7 : 8 * t + 8] > f32(0.5)
         local = jnp.where(active, r_ref[t, 0:EP, :].astype(f32), f32(0.0))
-        x_ref[at, :] = (local + y_ref[at, 0:BLK]).astype(bf16)
-        tail = jnp.where(lane_tail == 6, y_ref[at, BLK:WIDE], f32(0.0))
-        l_ref[at, HALF : HALF + 64] = pltpu.roll(tail, 122, 1)[:, 0:64].astype(bf16)
+        x_ref[at, 0:BLK] = (local + y_ref[at, 0:BLK]).astype(bf16)
+        x_ref[at, BLK:WIDE] = jnp.where(lane_tail == 6, y_ref[at, BLK:WIDE], f32(0.0)).astype(bf16)
 
     for side in range(2):
 
@@ -217,19 +215,24 @@
     scale = f32(1.0 / 4096.0)
     g_ref[...] = lax.dot_general(l_ref[...], x_ref[...], dims, preferred_element_type=f32) * scale
 
-    for side in range(2):
-
-        @pl.when(half == side)
-        def _():
-            for q in range(4):
-                first = 4 * SLICE * q + 2 * SLICE * side
-                rr_ref[:, 2 * SLICE * q : 2 * SLICE * (q + 1)] = g_ref[HALF : HALF + 8, first : first + 2 * SLICE]
-
+    row = lax.broadcasted_iota(jnp.int32, (SLICE, BLK), 0)
+    column = lax.broadcasted_iota(jnp.int32, (SLICE, BLK), 1) - SLICE * shard
+    carries = column == jnp.where(row == SLICE - 1, 0, row + 1)
+    mirrors = column == jnp.where(row == 0, SLICE - 1, row - 1)
+    code_ref[...] = jnp.where(carries, f32(1.0), jnp.where(mirrors, f32(2.0), f32(0.0))).astype(bf16)
     for s in range(8):
         slot, parity = lax.rem(turn + 4 - s // 2, 4), s % 2
-        beside = rr_ref[:, SLICE * s : SLICE * (s + 1)]
-        extra = jnp.concatenate([beside, jnp.zeros((8, BLK - SLICE), f32)], axis=1)
-        block = jnp.concatenate([g_ref[SLICE * s : SLICE * (s + 1), :], extra], axis=0)
+        at = slice(SLICE * s, SLICE * (s + 1))
+        start = 4 * SLICE * (s // 2) + SLICE * parity
+        low, top = start // 128 * 128, min(BLK, -(-(start + 3 * SLICE) // 128) * 128)
+        row = lax.broadcasted_iota(jnp.int32, (SLICE, top - low), 0)
+        column = lax.broadcasted_iota(jnp.int32, (SLICE, top - low), 1) + low
+        after = jnp.where(row == SLICE - 1, 0, row + 1)
+        near = jnp.where(
+            column == after + (start + 2 * SLICE * half), g_ref[at, BLK + 6 : BLK + 7], g_ref[at, low:top]
+        )
+        pieces = ([g_ref[at, 0:low]] if low else []) + [near] + ([g_ref[at, top:BLK]] if top < BLK else [])
+        block = jnp.concatenate(pieces, axis=1)
 
         @pl.when(core == parity)
         def _():
@@ -244,20 +247,20 @@
     return pl.pallas_call(
         normal_kernel,
         out_shape=(
-            jax.ShapeDtypeStruct((4, OUT_ROWS, BLK), f32),
-            jax.ShapeDtypeStruct((4, OUT_ROWS, BLK), bf16),
+            jax.ShapeDtypeStruct((4, SLICE, BLK), f32),
+            jax.ShapeDtypeStruct((4, SLICE, BLK), bf16),
+            jax.ShapeDtypeStruct((SLICE, BLK), bf16),
         ),
         in_specs=[pl.BlockSpec(memory_space=pltpu.VMEM)],
-        out_specs=(pl.BlockSpec(memory_space=pltpu.VMEM), pl.BlockSpec(memory_space=pltpu.VMEM)),
+        out_specs=(pl.BlockSpec(memory_space=pltpu.VMEM),) * 3,
         scratch_shapes=[
             pltpu.VMEM((8 * TS, 128), f32),
             pltpu.VMEM((8 * TS, WIDE), f32),
             pltpu.VMEM((TS * EP, 3 * AUG), bf16),
             pltpu.VMEM((TS * EP, WIDE), f32),
-            pltpu.VMEM((TS * EP, BLK), bf16),
-            pltpu.VMEM((TS * EP, HALF + 64), bf16),
-            pltpu.VMEM((HALF + 64, BLK), f32),
-            pltpu.VMEM((8, HALF), f32),
+            pltpu.VMEM((TS * EP, WIDE), bf16),
+            pltpu.VMEM((TS * EP, HALF), bf16),
+            pltpu.VMEM((HALF, WIDE), f32),
         ],
         compiler_params=pltpu.CompilerParams(vmem_limit_bytes=40 << 20),
         name="normal_rows",
@@ -273,7 +276,7 @@
         jnp.transpose(forcing[0], (1, 0, 2)),
     )
     received = lax.all_to_all(packed, "tm", split_axis=0, concat_axis=0, tiled=True)
-    keep, send = normals(received)
+    keep, send, code = normals(received)
     arcs, shards = lax.axis_size("arc"), lax.axis_size("tm")
     other_core = [(a * shards + t, (a ^ 1) * shards + t) for a in range(arcs) for t in range(shards)]
     arrived = lax.ppermute(send, ("arc", "tm"), other_core)
@@ -287,7 +290,11 @@
             z, c, y, h, odd = a // 2, a % 2, t // 4, t % 4 // 2, t % 2
             to_owner.append((a * shards + t, (2 * y + odd) * shards + (2 * y + 2 - z) % 4 * 4 + 2 * h + c))
     final = lax.ppermute(mine, ("arc", "tm"), to_owner).astype(f32)
-    return final[0:SLICE, :], final[SLICE, 0:SLICE]
+    kind = code.astype(f32)
+    carries, mirrors = kind == f32(1.0), kind == f32(2.0)
+    rhs = jnp.sum(jnp.where(carries, final, f32(0.0)), axis=1)
+    mirrored = jnp.sum(jnp.where(mirrors, final, f32(0.0)), axis=1, keepdims=True)
+    return jnp.where(carries, jnp.concatenate([mirrored[1:], mirrored[:1]], axis=0), final), rhs
 
 
 def solution(mesh):

time: 67.4 us -> 66 us (0.979)
  other arithmetic: 0.31 us -> 1.91 us
  local copies, waits for them, and re-layouts: 1.26 us -> 0.07 us
  blocking collectives: 43.6 us -> 42.8 us
  waiting for transfers between devices: 9.5 us -> 8.74 us
    select_n x0 -> x1, other arithmetic: none -> 0.84 us  [local(): jnp.where(carries, jnp.concatenate([mirrored[1:], mirrored[:1]], axis=0),...]
    all_to_all x1, blocking collectives: 17.2 us -> 16.4 us  [local(): lax.all_to_all(pair_sum, 'arc', split_axis=0, concat_axis=0, tiled=True,...]
    reduce_sum x0 -> x1, other arithmetic: none -> 0.7 us  [local(): rhs = jnp.sum(jnp.where(carries, final, f32(0.0)), axis=1)]
    slice x1, local copies, waits for them, and re-layouts: 0.75 us -> 0.07 us  [local(): mirrored[1:]]
where the time goes in v7:
time: 66 us; the launch traced here: 65.4 us
  blocking collectives  42.8 us (65%)
  waiting for transfers between devices  8.74 us (13%)
  Pallas kernels  7.45 us (11%)
  starting transfers between devices  3.14 us (5%)
  other arithmetic  1.91 us (3%)
  between operations  1.31 us (2%)
    all_to_all x1, blocking collectives, local(): lax.all_to_all(packed, 'tm', split_axis=0, concat_axis=0, tiled=True)  26.4 us
    all_to_all x1, blocking collectives, local(): lax.all_to_all(pair_sum, 'arc', split_axis=0, concat_axis=0, tiled=True,...  16.4 us
    ppermute x1, waiting for transfers between devices, local(): final = lax.ppermute(mine, ('arc', 'tm'), to_owner).astype(f32)  6.65 us
    pallas_call x1, Pallas kernels, normals(): pl.pallas_call(normal_kernel, out_shape=(jax.ShapeDtypeStruct((4, SLICE,...  4.8 us
    ppermute x1, starting transfers between devices, local(): final = lax.ppermute(mine, ('arc', 'tm'), to_owner).astype(f32)  3.06 us
    pallas_call x1, Pallas kernels, pack(): pl.pallas_call(pack_kernel, out_shape=jax.ShapeDtypeStruct((2 * n_blocks,...  2.65 us
    ppermute x1, waiting for transfers between devices, local(): arrived = lax.ppermute(send, ('arc', 'tm'), other_core)  2.1 us
  transfers between devices with their start and end apart: 2, of which 2 were waited for; matrix products, arithmetic and copies ran while one was open for 0% of the time, Pallas kernels for 0%

profile of v7, /device:TPU:24, one launch (start us, length us, event | category | flops | bytes accessed | tf_op | source)
XLA Modules:
  0.0 65.4 jit_solution(11807394606652167116)
XLA Ops:
  1.3 2.6 %pack_rows.1 = bf16[16,40,1152]{2,1,0:T(8,128)(2,1)S(1)} custom-call(s32[1,1]{1,0:T(1,128)S(6)} %copy.7.cnt_ref, f32[6,6,1,32]{3,2,1,0:T(1,128)} %bitcast.12, f32[6,1,32]{2,1,0:T(1,128)} %bitcast.13, f32[1,32]{1,0:T(1,128)} %ob_hbm.1, bf16[6,32,9216]{2,1,0:T(8,128)(2,1)} %bitcast.11), custom_call_target="tpu_custom_call" | custom-call | tf_op jit(solution)/shard_map/pack_rows/pallas_call | solution.py:100
  3.9 26.4 %all_to_all.10.r_ref = bf16[16,40,1152]{2,1,0:T(8,128)(2,1)S(1)} all-to-all(bf16[16,40,1152]{2,1,0:T(8,128)(2,1)S(1)} %pack_rows.1), channel_id=1, replica_groups=mesh['arc'=8,'tm'=16] {'tm'}, dimensions={0} | all-to-all | bytes 2949120 | tf_op jit(solution)/shard_map/all_to_all | solution.py:278
  30.3 4.8 %normal_rows.1 = (f32[4,72,1152]{2,1,0:T(8,128)S(1)}, bf16[4,72,1152]{2,1,0:T(8,128)(2,1)S(1)}, bf16[72,1152]{1,0:T(8,128)(2,1)S(1)}) custom-call(bf16[16,40,1152]{2,1,0:T(8,128)(2,1)S(1)} %all_to_all.10.r_ref), custom_call_target="tpu_custom_call" | custom-call | tf_op jit(solution)/shard_map/normal_rows/pallas_call | solution.py:247
  35.1 0.1 collective-permute-start
  35.2 2.1 %collective-permute-done = bf16[4,72,1152]{2,1,0:T(8,128)(2,1)S(1)} collective-permute-done((bf16[4,72,1152]{2,1,0:T(8,128)(2,1)S(1)}, bf16[4,72,1152]{2,1,0:T(8,128)(2,1)S(1)}, u32[]{:S(2)}, u32[]{:S(2)}) %collective-permute-start) | collective-permute-done | bytes 663584 | tf_op jit(solution)/shard_map/ppermute | solution.py:282
  37.3 0.2 add_convert_fusion
  37.5 16.4 %all_to_all.11 = bf16[4,72,1152]{2,1,0:T(8,128)(2,1)S(1)} all-to-all(bf16[4,72,1152]{2,1,0:T(8,128)(2,1)S(1)} %add_convert_fusion), channel_id=1, replica_groups={{0,32,64,96},{16,48,80,112},{1,33,65,97},{17,49,81,113},{2,34,66,98},{1..., dimensions={0} | all-to-all | bytes 1327104 | tf_op jit(solution)/shard_map/all_to_all | solution.py:285
  53.9 0.1 reduce_sum.30
  54.0 3.1 %collective-permute-start.1 = (bf16[72,1152]{1,0:T(8,128)(2,1)S(1)}, bf16[72,1152]{1,0:T(8,128)(2,1)S(1)}, u32[]{:S(2)}, u32[]{:S(2)}) collective-permute-start(bf16[72,1152]{1,0:T(8,128)(2,1)S(1)} %reduce_sum.30), channel_id=1, source_target_pairs={{0,8},{1,24},{2,10},{3,26},{4,32},{5,48},{6,34},{7,50},{8,72},{9,8... | collective-permute-start | bytes 497672 | tf_op jit(solution)/shard_map/ppermute | solution.py:292
  57.0 6.6 %collective-permute-done.1 = bf16[72,1152]{1,0:T(8,128)(2,1)S(1)} collective-permute-done((bf16[72,1152]{1,0:T(8,128)(2,1)S(1)}, bf16[72,1152]{1,0:T(8,128)(2,1)S(1)}, u32[]{:S(2)}, u32[]{:S(2)}) %collective-permute-start.1) | collective-permute-done | bytes 165920 | tf_op jit(solution)/shard_map/ppermute | solution.py:292
  63.7 0.7 %fusion.1 = (f32[72]{0:T(128)}, f32[72]{0:T(128)S(1)}) fusion(bf16[72,1152]{1,0:T(8,128)(2,1)S(1)} %collective-permute-done.1, bf16[72,1152]{1,0:T(8,128)(2,1)S(1)} %get-tuple-element.5), kind=kLoop, calls=%fused_computation.7 | loop fusion | flops 663408 | bytes 332352 | tf_op jit(solution)/shard_map/reduce_sum | solution.py:295
  64.4 0.1 slice_bitcast_fusion
  64.4 0.1 maximum_bitcast_fusion
  64.5 0.8 %convert_select_fusion.1 = f32[72,1152]{1,0:T(8,128)} fusion(bf16[72,1152]{1,0:T(8,128)(2,1)S(1)} %collective-permute-done.1, f32[72]{0:T(128)S(1)} %maximum_bitcast_fusion, bf16[72,1152]{1,0:T(8,128)(2,1)S(1)} %get-tuple-element.5), kind=kLoop, calls=%fused_computation.2 | loop fusion | flops 331776 | bytes 663840 | tf_op jit(solution)/shard_map/jit(_where)/select_n | solution.py:297
Async XLA Ops:
  35.1 2.2 %collective-permute-start = (bf16[4,72,1152]{2,1,0:T(8,128)(2,1)S(1)}, bf16[4,72,1152]{2,1,0:T(8,128)(2,1)S(1)}, u32[]{:S(2)}, u32[]{:S(2)}) collective-permute-start(bf16[4,72,1152]{2,1,0:T(8,128)(2,1)S(1)} %get-tuple-element.7), channel_id=1, source_target_pairs={{0,16},{1,17},{2,18},{3,19},{4,20},{5,21},{6,22},{7,23},{8,24},{9,... | collective-permute-start | bytes 1990664 | tf_op jit(solution)/shard_map/ppermute | solution.py:282
  54.0 9.7 %collective-permute-start.1 = (bf16[72,1152]{1,0:T(8,128)(2,1)S(1)}, bf16[72,1152]{1,0:T(8,128)(2,1)S(1)}, u32[]{:S(2)}, u32[]{:S(2)}) collective-permute-start(bf16[72,1152]{1,0:T(8,128)(2,1)S(1)} %reduce_sum.30), channel_id=1, source_target_pairs={{0,8},{1,24},{2,10},{3,26},{4,32},{5,48},{6,34},{7,50},{8,72},{9,8... | collective-permute-start | bytes 497672 | tf_op jit(solution)/shard_map/ppermute | solution.py:292

commit v8 on v7

--- a/solution.py
+++ b/solution.py
@@ -123,11 +123,39 @@
     return high, (x - high.astype(f32)).astype(bf16)
 
 
-def normal_kernel(r_ref, keep_ref, send_ref, code_ref, te_ref, in_ref, lead_ref, y_ref, x_ref, l_ref, g_ref):
+def position():
     shard = lax.axis_index("tm")
-    half = lax.div(lax.rem(shard, 4), 2)
-    turn = 2 * lax.div(shard, 4) + 2
-    core = lax.rem(lax.axis_index("arc"), 2)
+    return shard, lax.div(lax.rem(shard, 4), 2), 2 * lax.div(shard, 4) + 2, lax.rem(lax.axis_index("arc"), 2)
+
+
+def gram_slices(x_ref, l_ref, g_ref, out_ref, half, parity, turn):
+    for case in range(4):
+
+        @pl.when(2 * half + parity == case)
+        def _():
+            for q in range(4):
+                first = 4 * SLICE * q + SLICE * case
+                l_ref[:, SLICE * q : SLICE * (q + 1)] = x_ref[:, first : first + SLICE]
+
+    g_ref[...] = lax.dot_general(
+        l_ref[...], x_ref[...], (((0,), (0,)), ((), ())), preferred_element_type=f32
+    ) * f32(1.0 / 4096.0)
+    for q in range(4):
+        at = slice(SLICE * q, SLICE * (q + 1))
+        start = 4 * SLICE * q
+        low, top = start // 128 * 128, min(BLK, -(-(start + 4 * SLICE) // 128) * 128)
+        row = lax.broadcasted_iota(jnp.int32, (SLICE, top - low), 0)
+        column = lax.broadcasted_iota(jnp.int32, (SLICE, top - low), 1) + low
+        after = jnp.where(row == SLICE - 1, 0, row + 1)
+        near = jnp.where(
+            column == after + (start + SLICE * (2 * half + parity)), g_ref[at, BLK + 6 : BLK + 7], g_ref[at, low:top]
+        )
+        pieces = ([g_ref[at, 0:low]] if low else []) + [near] + ([g_ref[at, top:BLK]] if top < BLK else [])
+        out_ref[lax.rem(turn + 4 - q, 4)] = jnp.concatenate(pieces, axis=1).astype(out_ref.dtype)
+
+
+def normal_kernel(r_ref, send_ref, x_ref, te_ref, in_ref, lead_ref, y_ref, l_ref, g_ref):
+    shard, half, turn, core = position()
     dims = (((0,), (0,)), ((), ()))
     tails = [r_ref[t, 32:40, :].astype(f32) for t in range(TS)]
     for t in range(TS):
@@ -203,68 +231,51 @@
         x_ref[at, 0:BLK] = (local + y_ref[at, 0:BLK]).astype(bf16)
         x_ref[at, BLK:WIDE] = jnp.where(lane_tail == 6, y_ref[at, BLK:WIDE], f32(0.0)).astype(bf16)
 
-    for side in range(2):
-
-        @pl.when(half == side)
-        def _():
-            for q in range(4):
-                l_ref[:, 2 * SLICE * q : 2 * SLICE * (q + 1)] = x_ref[
-                    :, 4 * SLICE * q + 2 * SLICE * side : 4 * SLICE * q + 2 * SLICE * (side + 1)
-                ]
-
-    scale = f32(1.0 / 4096.0)
-    g_ref[...] = lax.dot_general(l_ref[...], x_ref[...], dims, preferred_element_type=f32) * scale
-
+    gram_slices(x_ref, l_ref, g_ref, send_ref, half, 1 - core, turn)
+
+
+def own_kernel(x_ref, keep_ref, code_ref, l_ref, g_ref):
+    shard, half, turn, core = position()
+    gram_slices(x_ref, l_ref, g_ref, keep_ref, half, core, turn)
     row = lax.broadcasted_iota(jnp.int32, (SLICE, BLK), 0)
     column = lax.broadcasted_iota(jnp.int32, (SLICE, BLK), 1) - SLICE * shard
     carries = column == jnp.where(row == SLICE - 1, 0, row + 1)
     mirrors = column == jnp.where(row == 0, SLICE - 1, row - 1)
     code_ref[...] = jnp.where(carries, f32(1.0), jnp.where(mirrors, f32(2.0), f32(0.0))).astype(bf16)
-    for s in range(8):
-        slot, parity = lax.rem(turn + 4 - s // 2, 4), s % 2
-        at = slice(SLICE * s, SLICE * (s + 1))
-        start = 4 * SLICE * (s // 2) + SLICE * parity
-        low, top = start // 128 * 128, min(BLK, -(-(start + 3 * SLICE) // 128) * 128)
-        row = lax.broadcasted_iota(jnp.int32, (SLICE, top - low), 0)
-        column = lax.broadcasted_iota(jnp.int32, (SLICE, top - low), 1) + low
-        after = jnp.where(row == SLICE - 1, 0, row + 1)
-        near = jnp.where(
-            column == after + (start + 2 * SLICE * half), g_ref[at, BLK + 6 : BLK + 7], g_ref[at, low:top]
-        )
-        pieces = ([g_ref[at, 0:low]] if low else []) + [near] + ([g_ref[at, top:BLK]] if top < BLK else [])
-        block = jnp.concatenate(pieces, axis=1)
-
-        @pl.when(core == parity)
-        def _():
-            keep_ref[slot] = block
-
-        @pl.when(core != parity)
-        def _():
-            send_ref[slot] = block.astype(bf16)
 
 
 def normals(received):
+    vmem = pl.BlockSpec(memory_space=pltpu.VMEM)
     return pl.pallas_call(
         normal_kernel,
-        out_shape=(
-            jax.ShapeDtypeStruct((4, SLICE, BLK), f32),
-            jax.ShapeDtypeStruct((4, SLICE, BLK), bf16),
-            jax.ShapeDtypeStruct((SLICE, BLK), bf16),
-        ),
-        in_specs=[pl.BlockSpec(memory_space=pltpu.VMEM)],
-        out_specs=(pl.BlockSpec(memory_space=pltpu.VMEM),) * 3,
+        out_shape=(jax.ShapeDtypeStruct((4, SLICE, BLK), bf16), jax.ShapeDtypeStruct((TS * EP, WIDE), bf16)),
+        in_specs=[vmem],
+        out_specs=(vmem, vmem),
         scratch_shapes=[
             pltpu.VMEM((8 * TS, 128), f32),
             pltpu.VMEM((8 * TS, WIDE), f32),
             pltpu.VMEM((TS * EP, 3 * AUG), bf16),
             pltpu.VMEM((TS * EP, WIDE), f32),
-            pltpu.VMEM((TS * EP, WIDE), bf16),
-            pltpu.VMEM((TS * EP, HALF), bf16),
-            pltpu.VMEM((HALF, WIDE), f32),
+            pltpu.VMEM((TS * EP, HALF // 2), bf16),
+            pltpu.VMEM((HALF // 2, WIDE), f32),
         ],
-        compiler_params=pltpu.CompilerParams(vmem_limit_bytes=40 << 20),
+        compiler_params=pltpu.CompilerParams(vmem_limit_bytes=32 << 20),
         name="normal_rows",
     )(received)
+
+
+def own_slices(rows):
+    vmem = pl.BlockSpec(memory_space=pltpu.VMEM)
+    return pl.pallas_call(
+        own_kernel,
+        out_shape=(jax.ShapeDtypeStruct((4, SLICE, BLK), f32), jax.ShapeDtypeStruct((SLICE, BLK), bf16)),
+        in_specs=[vmem],
+        out_specs=(vmem, vmem),
+        scratch_shapes=[pltpu.VMEM((TS * EP, HALF // 2), bf16), pltpu.VMEM((HALF // 2, WIDE), f32)],
+        cost_estimate=pl.CostEstimate(flops=2 * TS * EP * WIDE * HALF // 2, bytes_accessed=4 << 20, transcendentals=0),
+        compiler_params=pltpu.CompilerParams(vmem_limit_bytes=24 << 20),
+        name="own_slices",
+    )(rows)
 
 
 def local(transition, forcing, partials, observed, counts):
@@ -276,10 +287,11 @@
         jnp.transpose(forcing[0], (1, 0, 2)),
     )
     received = lax.all_to_all(packed, "tm", split_axis=0, concat_axis=0, tiled=True)
-    keep, send, code = normals(received)
+    send, rows = normals(received)
     arcs, shards = lax.axis_size("arc"), lax.axis_size("tm")
     other_core = [(a * shards + t, (a ^ 1) * shards + t) for a in range(arcs) for t in range(shards)]
     arrived = lax.ppermute(send, ("arc", "tm"), other_core)
+    keep, code = own_slices(rows)
     pair_sum = (keep + arrived.astype(f32)).astype(bf16)
     same_core = [[c + 2 * z for z in range(arcs // 2)] for c in range(2)]
     slices = lax.all_to_all(pair_sum, "arc", split_axis=0, concat_axis=0, tiled=True, axis_index_groups=same_core)

time: 66 us -> 64.9 us (0.983)
  waiting for transfers between devices: 8.74 us -> 7.79 us
    pallas_call x1, Pallas kernels: 4.8 us -> 3.68 us  [normals(): pl.pallas_call(normal_kernel, out_shape=(jax.ShapeDtypeStruct((4, SLICE,...]
    ppermute x1, waiting for transfers between devices: 2.1 us -> 1.14 us  [local(): arrived = lax.ppermute(send, ('arc', 'tm'), other_core)]
    pallas_call x0 -> x1, Pallas kernels: none -> 0.95 us  [own_slices(): pl.pallas_call(own_kernel, out_shape=(jax.ShapeDtypeStruct((4, SLICE, BLK...]
  transfers between devices with their start and end apart: 2 -> 2, of which waited for: 2 -> 2; matrix products, arithmetic and copies ran while one was open for 0% -> 0% of each run, Pallas kernels for 0% -> 1%
where the time goes in v8:
time: 64.9 us; the launch traced here: 64.2 us
  blocking collectives  42.8 us (66%)
  waiting for transfers between devices  7.79 us (12%)
  Pallas kernels  7.28 us (11%)
  starting transfers between devices  3.13 us (5%)
  other arithmetic  1.87 us (3%)
  between operations  1.32 us (2%)
    all_to_all x1, blocking collectives, local(): lax.all_to_all(packed, 'tm', split_axis=0, concat_axis=0, tiled=True)  26.4 us
    all_to_all x1, blocking collectives, local(): lax.all_to_all(pair_sum, 'arc', split_axis=0, concat_axis=0, tiled=True,...  16.4 us
    ppermute x1, waiting for transfers between devices, local(): final = lax.ppermute(mine, ('arc', 'tm'), to_owner).astype(f32)  6.65 us
    pallas_call x1, Pallas kernels, normals(): pl.pallas_call(normal_kernel, out_shape=(jax.ShapeDtypeStruct((4, SLICE,...  3.68 us
    ppermute x1, starting transfers between devices, local(): final = lax.ppermute(mine, ('arc', 'tm'), to_owner).astype(f32)  3.05 us
    pallas_call x1, Pallas kernels, pack(): pl.pallas_call(pack_kernel, out_shape=jax.ShapeDtypeStruct((2 * n_blocks,...  2.65 us
  transfers between devices with their start and end apart: 2, of which 2 were waited for; matrix products, arithmetic and copies ran while one was open for 0% of the time, Pallas kernels for 1%

profile of v8, /device:TPU:24, one launch (start us, length us, event | category | flops | bytes accessed | tf_op | source)
XLA Modules:
  0.0 64.2 jit_solution(5671612296744331716)
XLA Ops:
  1.3 2.6 %pack_rows.1 = bf16[16,40,1152]{2,1,0:T(8,128)(2,1)S(1)} custom-call(s32[1,1]{1,0:T(1,128)S(6)} %copy.7.cnt_ref, f32[6,6,1,32]{3,2,1,0:T(1,128)} %bitcast.12, f32[6,1,32]{2,1,0:T(1,128)} %bitcast.13, f32[1,32]{1,0:T(1,128)} %ob_hbm.1, bf16[6,32,9216]{2,1,0:T(8,128)(2,1)} %bitcast.11), custom_call_target="tpu_custom_call" | custom-call | tf_op jit(solution)/shard_map/pack_rows/pallas_call | solution.py:100
  3.9 26.4 %all_to_all.10.r_ref = bf16[16,40,1152]{2,1,0:T(8,128)(2,1)S(1)} all-to-all(bf16[16,40,1152]{2,1,0:T(8,128)(2,1)S(1)} %pack_rows.1), channel_id=1, replica_groups=mesh['arc'=8,'tm'=16] {'tm'}, dimensions={0} | all-to-all | bytes 2949120 | tf_op jit(solution)/shard_map/all_to_all | solution.py:289
  30.3 3.7 %normal_rows.1 = (bf16[4,72,1152]{2,1,0:T(8,128)(2,1)S(1)}, bf16[512,1280]{1,0:T(8,128)(2,1)S(1)}) custom-call(bf16[16,40,1152]{2,1,0:T(8,128)(2,1)S(1)} %all_to_all.10.r_ref), custom_call_target="tpu_custom_call" | custom-call | tf_op jit(solution)/shard_map/normal_rows/pallas_call | solution.py:249
  34.0 0.1 collective-permute-start
  34.1 0.9 %own_slices.1 = (f32[4,72,1152]{2,1,0:T(8,128)S(1)}, bf16[72,1152]{1,0:T(8,128)(2,1)S(1)}) custom-call(bf16[512,1280]{1,0:T(8,128)(2,1)S(1)} %get-tuple-element.6.x_ref), custom_call_target="tpu_custom_call" | custom-call | flops 377487360 | bytes 4194304 | tf_op jit(solution)/shard_map/own_slices/pallas_call | solution.py:269
  35.1 1.1 %collective-permute-done = bf16[4,72,1152]{2,1,0:T(8,128)(2,1)S(1)} collective-permute-done((bf16[4,72,1152]{2,1,0:T(8,128)(2,1)S(1)}, bf16[4,72,1152]{2,1,0:T(8,128)(2,1)S(1)}, u32[]{:S(2)}, u32[]{:S(2)}) %collective-permute-start) | collective-permute-done | bytes 663584 | tf_op jit(solution)/shard_map/ppermute | solution.py:293
  36.2 0.1 add_convert_fusion
  36.3 16.4 %all_to_all.11 = bf16[4,72,1152]{2,1,0:T(8,128)(2,1)S(1)} all-to-all(bf16[4,72,1152]{2,1,0:T(8,128)(2,1)S(1)} %add_convert_fusion), channel_id=1, replica_groups={{0,32,64,96},{16,48,80,112},{1,33,65,97},{17,49,81,113},{2,34,66,98},{1..., dimensions={0} | all-to-all | bytes 1327104 | tf_op jit(solution)/shard_map/all_to_all | solution.py:297
  52.7 0.1 reduce_sum.30
  52.8 3.0 %collective-permute-start.1 = (bf16[72,1152]{1,0:T(8,128)(2,1)S(1)}, bf16[72,1152]{1,0:T(8,128)(2,1)S(1)}, u32[]{:S(2)}, u32[]{:S(2)}) collective-permute-start(bf16[72,1152]{1,0:T(8,128)(2,1)S(1)} %reduce_sum.30), channel_id=1, source_target_pairs={{0,8},{1,24},{2,10},{3,26},{4,32},{5,48},{6,34},{7,50},{8,72},{9,8... | collective-permute-start | bytes 497672 | tf_op jit(solution)/shard_map/ppermute | solution.py:304
  55.9 6.7 %collective-permute-done.1 = bf16[72,1152]{1,0:T(8,128)(2,1)S(1)} collective-permute-done((bf16[72,1152]{1,0:T(8,128)(2,1)S(1)}, bf16[72,1152]{1,0:T(8,128)(2,1)S(1)}, u32[]{:S(2)}, u32[]{:S(2)}) %collective-permute-start.1) | collective-permute-done | bytes 165920 | tf_op jit(solution)/shard_map/ppermute | solution.py:304
  62.5 0.7 %fusion.1 = (f32[72]{0:T(128)}, f32[72]{0:T(128)S(1)}) fusion(bf16[72,1152]{1,0:T(8,128)(2,1)S(1)} %collective-permute-done.1, bf16[72,1152]{1,0:T(8,128)(2,1)S(1)} %get-tuple-element.7), kind=kLoop, calls=%fused_computation.7 | loop fusion | flops 663408 | bytes 332352 | tf_op jit(solution)/shard_map/reduce_sum | solution.py:307
  63.2 0.1 slice_bitcast_fusion
  63.3 0.1 maximum_bitcast_fusion
  63.4 0.8 %convert_select_fusion.1 = f32[72,1152]{1,0:T(8,128)} fusion(bf16[72,1152]{1,0:T(8,128)(2,1)S(1)} %collective-permute-done.1, f32[72]{0:T(128)S(1)} %maximum_bitcast_fusion, bf16[72,1152]{1,0:T(8,128)(2,1)S(1)} %get-tuple-element.7), kind=kLoop, calls=%fused_computation.2 | loop fusion | flops 331776 | bytes 663840 | tf_op jit(solution)/shard_map/jit(_where)/select_n | solution.py:309
Async XLA Ops:
  34.0 2.2 %collective-permute-start = (bf16[4,72,1152]{2,1,0:T(8,128)(2,1)S(1)}, bf16[4,72,1152]{2,1,0:T(8,128)(2,1)S(1)}, u32[]{:S(2)}, u32[]{:S(2)}) collective-permute-start(bf16[4,72,1152]{2,1,0:T(8,128)(2,1)S(1)} %get-tuple-element.9), channel_id=1, source_target_pairs={{0,16},{1,17},{2,18},{3,19},{4,20},{5,21},{6,22},{7,23},{8,24},{9,... | collective-permute-start | bytes 1990664 | tf_op jit(solution)/shard_map/ppermute | solution.py:293
  52.8 9.7 %collective-permute-start.1 = (bf16[72,1152]{1,0:T(8,128)(2,1)S(1)}, bf16[72,1152]{1,0:T(8,128)(2,1)S(1)}, u32[]{:S(2)}, u32[]{:S(2)}) collective-permute-start(bf16[72,1152]{1,0:T(8,128)(2,1)S(1)} %reduce_sum.30), channel_id=1, source_target_pairs={{0,8},{1,24},{2,10},{3,26},{4,32},{5,48},{6,34},{7,50},{8,72},{9,8... | collective-permute-start | bytes 497672 | tf_op jit(solution)/shard_map/ppermute | solution.py:304

commit v9 on v8

--- a/solution.py
+++ b/solution.py
@@ -125,7 +125,7 @@
 
 def position():
     shard = lax.axis_index("tm")
-    return shard, lax.div(lax.rem(shard, 4), 2), 2 * lax.div(shard, 4) + 2, lax.rem(lax.axis_index("arc"), 2)
+    return shard, lax.div(lax.rem(shard, 4), 2), 2 * lax.div(shard, 4) + 6 - lax.div(lax.axis_index("arc"), 2), lax.rem(lax.axis_index("arc"), 2)
 
 
 def gram_slices(x_ref, l_ref, g_ref, out_ref, half, parity, turn):
@@ -292,16 +292,16 @@
     other_core = [(a * shards + t, (a ^ 1) * shards + t) for a in range(arcs) for t in range(shards)]
     arrived = lax.ppermute(send, ("arc", "tm"), other_core)
     keep, code = own_slices(rows)
-    pair_sum = (keep + arrived.astype(f32)).astype(bf16)
-    same_core = [[c + 2 * z for z in range(arcs // 2)] for c in range(2)]
-    slices = lax.all_to_all(pair_sum, "arc", split_axis=0, concat_axis=0, tiled=True, axis_index_groups=same_core)
-    mine = jnp.sum(slices.astype(f32), axis=0).astype(bf16)
-    to_owner = []
-    for a in range(arcs):
-        for t in range(shards):
-            z, c, y, h, odd = a // 2, a % 2, t // 4, t % 4 // 2, t % 2
-            to_owner.append((a * shards + t, (2 * y + odd) * shards + (2 * y + 2 - z) % 4 * 4 + 2 * h + c))
-    final = lax.ppermute(mine, ("arc", "tm"), to_owner).astype(f32)
+    final = None
+    for k in range(3, -1, -1):
+        pair_sum = (keep[k] + arrived[k].astype(f32)).astype(bf16)
+        to_owner = []
+        for a in range(arcs):
+            for t in range(shards):
+                z, c, y, h, odd = a // 2, a % 2, t // 4, t % 4 // 2, t % 2
+                to_owner.append((a * shards + t, (2 * y + odd) * shards + (2 * y + 2 - z - k) % 4 * 4 + 2 * h + c))
+        part = lax.ppermute(pair_sum, ("arc", "tm"), to_owner).astype(f32)
+        final = part if final is None else final + part
     kind = code.astype(f32)
     carries, mirrors = kind == f32(1.0), kind == f32(2.0)
     rhs = jnp.sum(jnp.where(carries, final, f32(0.0)), axis=1)

time: 64.9 us -> 59.3 us (0.914)
  the two profiles are of different devices: /device:TPU:24 before, /device:TPU:64 now
where the time goes in v9:
time: 59.3 us; the launch traced here: 59.2 us
  blocking collectives  28.6 us (48%)
  waiting for transfers between devices  11.3 us (19%)
  starting transfers between devices  8.79 us (15%)
  Pallas kernels  7.28 us (12%)
  other arithmetic  1.85 us (3%)
  between operations  1.33 us (2%)
    all_to_all x1, blocking collectives, local(): lax.all_to_all(packed, 'tm', split_axis=0, concat_axis=0, tiled=True)  28.6 us
    ppermute x4, waiting for transfers between devices, local(): part = lax.ppermute(pair_sum, ('arc', 'tm'), to_owner).astype(f32)  10.1 us
    ppermute x4, starting transfers between devices, local(): part = lax.ppermute(pair_sum, ('arc', 'tm'), to_owner).astype(f32)  8.7 us
    pallas_call x1, Pallas kernels, normals(): pl.pallas_call(normal_kernel, out_shape=(jax.ShapeDtypeStruct((4, SLICE,...  3.68 us
    pallas_call x1, Pallas kernels, pack(): pl.pallas_call(pack_kernel, out_shape=jax.ShapeDtypeStruct((2 * n_blocks,...  2.65 us
  transfers between devices with their start and end apart: 5, of which 3 were waited for; matrix products, arithmetic and copies ran while one was open for 0% of the time, Pallas kernels for 2%

profile of v9, /device:TPU:64, one launch (start us, length us, event | category | flops | bytes accessed | tf_op | source)
XLA Modules:
  0.0 59.2 jit_solution(9808619406900221866)
XLA Ops:
  1.3 2.6 %pack_rows.1 = bf16[16,40,1152]{2,1,0:T(8,128)(2,1)S(1)} custom-call(s32[1,1]{1,0:T(1,128)S(6)} %copy.7.cnt_ref, f32[6,6,1,32]{3,2,1,0:T(1,128)} %bitcast.20, f32[6,1,32]{2,1,0:T(1,128)} %bitcast.21, f32[1,32]{1,0:T(1,128)} %ob_hbm.1, bf16[6,32,9216]{2,1,0:T(8,128)(2,1)} %bitcast.19), custom_call_target="tpu_custom_call" | custom-call | tf_op jit(solution)/shard_map/pack_rows/pallas_call | solution.py:100
  3.9 28.6 %all_to_all.5.r_ref = bf16[16,40,1152]{2,1,0:T(8,128)(2,1)S(1)} all-to-all(bf16[16,40,1152]{2,1,0:T(8,128)(2,1)S(1)} %pack_rows.1), channel_id=1, replica_groups=mesh['arc'=8,'tm'=16] {'tm'}, dimensions={0} | all-to-all | bytes 2949120 | tf_op jit(solution)/shard_map/all_to_all | solution.py:289
  32.5 3.7 %normal_rows.1 = (bf16[4,72,1152]{2,1,0:T(8,128)(2,1)S(1)}, bf16[512,1280]{1,0:T(8,128)(2,1)S(1)}) custom-call(bf16[16,40,1152]{2,1,0:T(8,128)(2,1)S(1)} %all_to_all.5.r_ref), custom_call_target="tpu_custom_call" | custom-call | tf_op jit(solution)/shard_map/normal_rows/pallas_call | solution.py:249
  36.2 0.1 collective-permute-start
  36.3 0.9 %own_slices.1 = (f32[4,72,1152]{2,1,0:T(8,128)S(1)}, bf16[72,1152]{1,0:T(8,128)(2,1)S(1)}) custom-call(bf16[512,1280]{1,0:T(8,128)(2,1)S(1)} %get-tuple-element.6.x_ref), custom_call_target="tpu_custom_call" | custom-call | flops 377487360 | bytes 4194304 | tf_op jit(solution)/shard_map/own_slices/pallas_call | solution.py:269
  37.2 1.1 %collective-permute-done = bf16[4,72,1152]{2,1,0:T(8,128)(2,1)S(1)} collective-permute-done((bf16[4,72,1152]{2,1,0:T(8,128)(2,1)S(1)}, bf16[4,72,1152]{2,1,0:T(8,128)(2,1)S(1)}, u32[]{:S(2)}, u32[]{:S(2)}) %collective-permute-start) | collective-permute-done | bytes 663584 | tf_op jit(solution)/shard_map/ppermute | solution.py:293
  38.4 0.1 fusion
  38.5 0.1 collective-permute-start.1
  38.6 0.5 collective-permute-start.4
  39.1 5.4 %collective-permute-start.3 = (bf16[72,1152]{1,0:T(8,128)(2,1)S(1)}, bf16[72,1152]{1,0:T(8,128)(2,1)S(1)}, u32[]{:S(2)}, u32[]{:S(2)}) collective-permute-start(bf16[72,1152]{1,0:T(8,128)(2,1)S(1)} %get-tuple-element.14), channel_id=1, source_target_pairs={{0,4},{1,20},{2,6},{3,22},{4,44},{5,60},{6,46},{7,62},{8,68},{9,84... | collective-permute-start | bytes 497672 | tf_op jit(solution)/shard_map/ppermute | solution.py:303
  44.4 2.8 %collective-permute-start.2 = (bf16[72,1152]{1,0:T(8,128)(2,1)S(1)}, bf16[72,1152]{1,0:T(8,128)(2,1)S(1)}, u32[]{:S(2)}, u32[]{:S(2)}) collective-permute-start(bf16[72,1152]{1,0:T(8,128)(2,1)S(1)} %get-tuple-element.15), channel_id=1, source_target_pairs={{0,0},{1,16},{2,2},{3,18},{4,40},{5,56},{6,42},{7,58},{8,64},{9,80... | collective-permute-start | bytes 497672 | tf_op jit(solution)/shard_map/ppermute | solution.py:303
  47.2 4.1 %collective-permute-done.1 = bf16[72,1152]{1,0:T(8,128)(2,1)S(1)} collective-permute-done((bf16[72,1152]{1,0:T(8,128)(2,1)S(1)}, bf16[72,1152]{1,0:T(8,128)(2,1)S(1)}, u32[]{:S(2)}, u32[]{:S(2)}) %collective-permute-start.1) | collective-permute-done | bytes 165920 | tf_op jit(solution)/shard_map/ppermute | solution.py:303
  51.3 0.0 collective-permute-done.4
  51.3 0.0 collective-permute-done.3
  51.3 6.1 %collective-permute-done.2 = bf16[72,1152]{1,0:T(8,128)(2,1)S(1)} collective-permute-done((bf16[72,1152]{1,0:T(8,128)(2,1)S(1)}, bf16[72,1152]{1,0:T(8,128)(2,1)S(1)}, u32[]{:S(2)}, u32[]{:S(2)}) %collective-permute-start.2) | collective-permute-done | bytes 165920 | tf_op jit(solution)/shard_map/ppermute | solution.py:303
  57.3 0.8 %select_reduce_fusion = (f32[72]{0:T(128)}, f32[72]{0:T(128)S(1)}) fusion(bf16[72,1152]{1,0:T(8,128)(2,1)S(1)} %get-tuple-element.7, bf16[72,1152]{1,0:T(8,128)(2,1)S(1)} %collective-permute-done.4, bf16[72,1152]{1,0:T(8,128)(2,1)S(1)} %collective-permute-done.3, bf16[72,1152]{1,0:T(8,128)(2,1)S(1)} %collective-permute-done.2, ...), kind=kLoop, calls=%fused_computation.2 | loop fusion | flops 1161072 | bytes 830016 | tf_op jit(solution)/shard_map/reduce_sum | solution.py:307
  58.1 0.1 slice_bitcast_fusion
  58.2 0.1 maximum_bitcast_fusion
  58.3 0.9 %broadcast_select_fusion = f32[72,1152]{1,0:T(8,128)} fusion(f32[72]{0:T(128)S(1)} %maximum_bitcast_fusion, bf16[72,1152]{1,0:T(8,128)(2,1)S(1)} %get-tuple-element.7, bf16[72,1152]{1,0:T(8,128)(2,1)S(1)} %collective-permute-done.4, bf16[72,1152]{1,0:T(8,128)(2,1)S(1)} %collective-permute-done.3, bf16[72,1152]{1,0:T(8,128)(2,1)S(1)} %collective-permute-done.2, ...), kind=kLoop, calls=%fused_computation.13 | loop fusion | flops 829440 | bytes 1161504 | tf_op jit(solution)/shard_map/jit(_where)/select_n | solution.py:309
Async XLA Ops:
  36.2 2.2 %collective-permute-start = (bf16[4,72,1152]{2,1,0:T(8,128)(2,1)S(1)}, bf16[4,72,1152]{2,1,0:T(8,128)(2,1)S(1)}, u32[]{:S(2)}, u32[]{:S(2)}) collective-permute-start(bf16[4,72,1152]{2,1,0:T(8,128)(2,1)S(1)} %get-tuple-element.9), channel_id=1, source_target_pairs={{0,16},{1,17},{2,18},{3,19},{4,20},{5,21},{6,22},{7,23},{8,24},{9,... | collective-permute-start | bytes 1990664 | tf_op jit(solution)/shard_map/ppermute | solution.py:293
  38.5 12.8 %collective-permute-start.1 = (bf16[72,1152]{1,0:T(8,128)(2,1)S(1)}, bf16[72,1152]{1,0:T(8,128)(2,1)S(1)}, u32[]{:S(2)}, u32[]{:S(2)}) collective-permute-start(bf16[72,1152]{1,0:T(8,128)(2,1)S(1)} %get-tuple-element.12), channel_id=1, source_target_pairs={{0,12},{1,28},{2,14},{3,30},{4,36},{5,52},{6,38},{7,54},{8,76},{9,... | collective-permute-start | bytes 497672 | tf_op jit(solution)/shard_map/ppermute | solution.py:303
  38.6 12.7 %collective-permute-start.4 = (bf16[72,1152]{1,0:T(8,128)(2,1)S(1)}, bf16[72,1152]{1,0:T(8,128)(2,1)S(1)}, u32[]{:S(2)}, u32[]{:S(2)}) collective-permute-start(bf16[72,1152]{1,0:T(8,128)(2,1)S(1)} %get-tuple-element.13), channel_id=1, source_target_pairs={{0,8},{1,24},{2,10},{3,26},{4,32},{5,48},{6,34},{7,50},{8,72},{9,8... | collective-permute-start | bytes 497672 | tf_op jit(solution)/shard_map/ppermute | solution.py:303
  39.1 12.2 %collective-permute-start.3 = (bf16[72,1152]{1,0:T(8,128)(2,1)S(1)}, bf16[72,1152]{1,0:T(8,128)(2,1)S(1)}, u32[]{:S(2)}, u32[]{:S(2)}) collective-permute-start(bf16[72,1152]{1,0:T(8,128)(2,1)S(1)} %get-tuple-element.14), channel_id=1, source_target_pairs={{0,4},{1,20},{2,6},{3,22},{4,44},{5,60},{6,46},{7,62},{8,68},{9,84... | collective-permute-start | bytes 497672 | tf_op jit(solution)/shard_map/ppermute | solution.py:303
  44.4 12.9 %collective-permute-start.2 = (bf16[72,1152]{1,0:T(8,128)(2,1)S(1)}, bf16[72,1152]{1,0:T(8,128)(2,1)S(1)}, u32[]{:S(2)}, u32[]{:S(2)}) collective-permute-start(bf16[72,1152]{1,0:T(8,128)(2,1)S(1)} %get-tuple-element.15), channel_id=1, source_target_pairs={{0,0},{1,16},{2,2},{3,18},{4,40},{5,56},{6,42},{7,58},{8,64},{9,80... | collective-permute-start | bytes 497672 | tf_op jit(solution)/shard_map/ppermute | solution.py:303
